TPU v7x, 256 devices: a whole 4x4x8 slice. The times are simulated.
256 devices in a mesh: dp: 4 (over x), seq: 64 (over y, z, core).
Axes of the slice: x: 4, y: 4, z: 8, core: 2. Of those that a mesh axis runs over, the one named last changes fastest.
Arguments:
- queries: bfloat16 [32768, 32, 128], P(('dp', 'seq')), parts along dimension 0, may hold values from -6 to 6
- keys: bfloat16 [32768, 4, 128], P(('dp', 'seq')), parts along dimension 0, may hold values from -6 to 6
- values: bfloat16 [32768, 4, 128], P(('dp', 'seq')), parts along dimension 0, may hold values from -6 to 6
- attn_out: bfloat16 [32768, 32, 128], P(('dp', 'seq')), parts along dimension 0, may hold values from -6 to 6
- out_grad: bfloat16 [32768, 32, 128], P(('dp', 'seq')), parts along dimension 0, may hold values from -1.5 to 1.5
- log_sums: float32 [32, 32768], P(None, ('dp', 'seq')), parts along dimension 1, may hold values from 2 to 4
- doc_ids: int32 [32768], P('dp'), parts along dimension 0, may hold values from 0 to 31, never falling along the last dimension, each value on 1 to 512 neighbouring positions
Outputs:
- query_grad: bfloat16 [32768, 32, 128], P(('dp', 'seq')), parts along dimension 0
- key_grad: bfloat16 [32768, 4, 128], P(('dp', 'seq')), parts along dimension 0
- value_grad: bfloat16 [32768, 4, 128], P(('dp', 'seq')), parts along dimension 0
There are 4 independent parts, one for each index of `dp`. A program takes and returns all parts, laid end to end along the dimension named above; each array names one. Nothing has to cross between parts.
Inputs may be any that keep to these rules, and one draw needn't show every extreme that they name: `doc_ids`: document numbers never fall along the sequence; each document holds 1 to 512 positions, and one holds exactly 512.
All inputs are finite; a program needn't handle non-finite values.
Results may differ from a plain program's by a relative error of at most 0.009.
Values may be sent and summed in bfloat16 or wider, within the bound.
A program may use at most 64 MiB of HBM per device.

v0:
```python
import jax
import jax.numpy as jnp
from jax import lax
from jax.sharding import PartitionSpec as P

REACH = 4


def from_behind(value, axis, steps):
    count = lax.axis_size(axis)
    initial, last = (max(0, -steps), min(count, count - steps))
    return lax.ppermute(value, axis, [(source, source + steps) for source in range(initial, last)])


def on_device(queries, keys, values, attn_out, out_grad, log_sums, doc_ids):
    width = queries.shape[0]
    heads = queries.shape[1]
    head_size = queries.shape[2]
    kv_count = keys.shape[1]
    group = heads // kv_count
    scale = head_size ** (-0.5)
    shard = lax.axis_index("seq")
    delta = jnp.sum(out_grad.astype(jnp.float32) * attn_out.astype(jnp.float32), axis=-1).T.reshape(
        kv_count, group, width
    )
    log_blk = log_sums.reshape(kv_count, group, width)
    query_grp = queries.reshape(width, kv_count, group, head_size)
    grad_grp = out_grad.reshape(width, kv_count, group, head_size)
    offsets = jnp.arange(width, dtype=jnp.int32)
    query_pos = shard * width + offsets
    query_doc = lax.dynamic_slice_in_dim(doc_ids, shard * width, width, 0)

    def live_mask(distance):
        key_start = (shard - distance) * width
        key_pos = key_start + offsets
        key_doc = lax.dynamic_slice_in_dim(doc_ids, jnp.maximum(key_start, 0), width, 0)
        return (
            (key_pos[None, :] <= query_pos[:, None])
            & (key_doc[None, :] == query_doc[:, None])
            & (key_pos[None, :] >= 0)
        )

    def gradients(key_blk, val_blk, live):
        scores = (
            jnp.einsum("tkgd,skd->kgts", query_grp, key_blk, preferred_element_type=jnp.float32)
            * scale
        )
        probs = jnp.where(live, jnp.exp(scores - log_blk[..., None]), 0.0)
        dprobs = jnp.einsum("tkgd,skd->kgts", grad_grp, val_blk, preferred_element_type=jnp.float32)
        dscores = (probs * (dprobs - delta[..., None])).astype(jnp.bfloat16)
        probs_low = probs.astype(jnp.bfloat16)
        query_part = (
            jnp.einsum("kgts,skd->tkgd", dscores, key_blk, preferred_element_type=jnp.float32)
            * scale
        )
        key_part = (
            jnp.einsum("kgts,tkgd->skd", dscores, query_grp, preferred_element_type=jnp.float32)
            * scale
        )
        val_part = jnp.einsum(
            "kgts,tkgd->skd", probs_low, grad_grp, preferred_element_type=jnp.float32
        )
        return (query_part, key_part.astype(jnp.bfloat16), val_part.astype(jnp.bfloat16))

    key_list = []
    val_list = []
    for distance in range(1, REACH + 1):
        key_got, val_got = from_behind((keys, values), "seq", distance)
        key_list.append(key_got)
        val_list.append(val_got)
    key_far = jnp.stack(key_list)
    val_far = jnp.stack(val_list)
    query_total, key_own, val_own = gradients(keys, values, live_mask(0))
    key_parts = []
    val_parts = []
    for distance in range(1, REACH + 1):
        live = live_mask(distance)
        key_blk = key_far[distance - 1]
        val_blk = val_far[distance - 1]
        query_part, key_part, val_part = gradients(key_blk, val_blk, live)
        query_total = query_total + query_part
        key_parts.append(key_part)
        val_parts.append(val_part)
    key_stack = jnp.stack(key_parts)
    val_stack = jnp.stack(val_parts)
    key_total = key_own.astype(jnp.float32)
    val_total = val_own.astype(jnp.float32)
    for distance in range(1, REACH + 1):
        key_back, val_back = from_behind(
            (key_stack[distance - 1], val_stack[distance - 1]), "seq", -distance
        )
        key_total = key_total + key_back.astype(jnp.float32)
        val_total = val_total + val_back.astype(jnp.float32)
    query_grad = query_total.reshape(width, heads, head_size).astype(jnp.bfloat16)
    return (query_grad, key_total.astype(jnp.bfloat16), val_total.astype(jnp.bfloat16))


def solution(mesh):
    placed = (
        P(("dp", "seq"), None, None),
        P(("dp", "seq"), None, None),
        P(("dp", "seq"), None, None),
        P(("dp", "seq"), None, None),
        P(("dp", "seq"), None, None),
        P(None, ("dp", "seq")),
        P("dp"),
    )
    return jax.shard_map(
        on_device,
        mesh=mesh,
        in_specs=placed,
        out_specs=(
            P(("dp", "seq"), None, None),
            P(("dp", "seq"), None, None),
            P(("dp", "seq"), None, None),
        ),
        check_vma=False,
    )
```

profile of v0, /device:TPU:47, one launch (start us, length us, event | category | flops | bytes accessed | tf_op | source)
XLA Modules:
  0.0 96.0 jit_solution(13420131180888751660)
XLA Ops:
  0.6 0.0 copy-start
  0.6 0.0 copy-start.3
  0.7 1.0 %copy.98 = bf16[128,4,128]{2,0,1:T(8,128)(2,1)S(1)} copy(bf16[128,4,128]{2,1,0:T(4,128)(2,1)} %param.9) | data formatting | bytes 262144 | tf_op args[2]
  1.7 4.9 %collective-permute-start.7 = (bf16[128,4,128]{2,0,1:T(8,128)(2,1)S(1)}, bf16[128,4,128]{2,0,1:T(8,128)(2,1)S(1)}, u32[]{:S(2)}, u32[]{:S(2)}) collective-permute-start(bf16[128,4,128]{2,0,1:T(8,128)(2,1)S(1)} %copy.98), channel_id=1, source_target_pairs={{0,4},{1,5},{2,6},{3,7},{4,8},{5,9},{6,10},{7,11},{8,12},{9,13},{1... | collective-permute-start | bytes 393224 | tf_op jit(solution)/shard_map/ppermute | solution.py:12
  6.6 6.1 %collective-permute-start.5 = (bf16[128,4,128]{2,0,1:T(8,128)(2,1)S(1)}, bf16[128,4,128]{2,0,1:T(8,128)(2,1)S(1)}, u32[]{:S(2)}, u32[]{:S(2)}) collective-permute-start(bf16[128,4,128]{2,0,1:T(8,128)(2,1)S(1)} %copy.98), channel_id=1, source_target_pairs={{0,3},{1,4},{2,5},{3,6},{4,7},{5,8},{6,9},{7,10},{8,11},{9,12},{10... | collective-permute-start | bytes 393224 | tf_op jit(solution)/shard_map/ppermute | solution.py:12
  12.7 2.6 %collective-permute-start.3 = (bf16[128,4,128]{2,0,1:T(8,128)(2,1)S(1)}, bf16[128,4,128]{2,0,1:T(8,128)(2,1)S(1)}, u32[]{:S(2)}, u32[]{:S(2)}) collective-permute-start(bf16[128,4,128]{2,0,1:T(8,128)(2,1)S(1)} %copy.98), channel_id=1, source_target_pairs={{0,2},{1,3},{2,4},{3,5},{4,6},{5,7},{6,8},{7,9},{8,10},{9,11},{10,... | collective-permute-start | bytes 393224 | tf_op jit(solution)/shard_map/ppermute | solution.py:12
  15.3 1.9 %collective-permute-start.1 = (bf16[128,4,128]{2,0,1:T(8,128)(2,1)S(1)}, bf16[128,4,128]{2,0,1:T(8,128)(2,1)S(1)}, u32[]{:S(2)}, u32[]{:S(2)}) collective-permute-start(bf16[128,4,128]{2,0,1:T(8,128)(2,1)S(1)} %copy.98), channel_id=1, source_target_pairs={{0,1},{1,2},{2,3},{3,4},{4,5},{5,6},{6,7},{7,8},{8,9},{9,10},{10,1... | collective-permute-start | bytes 393224 | tf_op jit(solution)/shard_map/ppermute | solution.py:12
  17.2 0.9 copy.96
  18.2 3.0 %collective-permute-start = (bf16[128,4,128]{2,0,1:T(8,128)(2,1)S(1)}, bf16[128,4,128]{2,0,1:T(8,128)(2,1)S(1)}, u32[]{:S(2)}, u32[]{:S(2)}) collective-permute-start(bf16[128,4,128]{2,0,1:T(8,128)(2,1)S(1)} %copy.96), channel_id=1, source_target_pairs={{0,1},{1,2},{2,3},{3,4},{4,5},{5,6},{6,7},{7,8},{8,9},{9,10},{10,1... | collective-permute-start | bytes 393224 | tf_op jit(solution)/shard_map/ppermute | solution.py:12
  21.3 2.2 %multiply_reduce_fusion = f32[128,32]{1,0:T(8,128)S(1)} fusion(bf16[128,32,128]{2,1,0:T(8,128)(2,1)} %param.10, bf16[128,32,128]{2,1,0:T(8,128)(2,1)} %param.11), kind=kLoop, calls=%fused_computation.31 | loop fusion | flops 2093056 | bytes 2113536 | tf_op jit(solution)/shard_map/reduce_sum | solution.py:23
  23.5 0.0 copy-start.1
  23.5 0.0 copy-start.2
  23.5 0.1 copy.93
  23.5 1.0 %fusion.98 = (s32[128]{0:T(128)S(1)}, s32[128]{0:T(128)S(1)}, s32[128]{0:T(128)S(1)}, s32[128]{0:T(128)S(1)}, s32[128]{0:T(128)S(1)}, /*index=5*/s32[128]{0:T(128)S(1)}, s32[128]{0:T(128)S(1)}) fusion(s32[8192]{0:T(1024)} %param.13, s32[]{:T(128)S(6)} %max.19, s32[]{:T(128)S(6)} %max.17, s32[]{:T(128)S(6)} %max.16, s32[]{:T(128)S(6)} %select_n.24, ...), kind=kLoop, calls=%fused_computation.131 | loop fusion | flops 128 | bytes 6684 | tf_op jit(solution)/shard_map/dynamic_slice | solution.py:36
  24.6 0.3 and_and_fusion
  24.9 0.8 fusion.19
  25.7 0.6 fusion.17
  26.4 0.5 fusion.71
  26.9 0.0 collective-permute-done
  26.9 1.9 %collective-permute-start.2 = (bf16[128,4,128]{2,0,1:T(8,128)(2,1)S(1)}, bf16[128,4,128]{2,0,1:T(8,128)(2,1)S(1)}, u32[]{:S(2)}, u32[]{:S(2)}) collective-permute-start(bf16[128,4,128]{2,0,1:T(8,128)(2,1)S(1)} %copy.96), channel_id=1, source_target_pairs={{0,2},{1,3},{2,4},{3,5},{4,6},{5,7},{6,8},{7,9},{8,10},{9,11},{10,... | collective-permute-start | bytes 393224 | tf_op jit(solution)/shard_map/ppermute | solution.py:12
  28.8 0.8 fusion.15
  29.6 0.6 fusion.46
  30.2 3.8 %collective-permute-done.2 = bf16[128,4,128]{2,0,1:T(8,128)(2,1)S(1)} collective-permute-done((bf16[128,4,128]{2,0,1:T(8,128)(2,1)S(1)}, bf16[128,4,128]{2,0,1:T(8,128)(2,1)S(1)}, u32[]{:S(2)}, u32[]{:S(2)}) %collective-permute-start.2) | collective-permute-done | bytes 131104 | tf_op jit(solution)/shard_map/ppermute | solution.py:12
  34.0 1.9 %collective-permute-start.6 = (bf16[128,4,128]{2,0,1:T(8,128)(2,1)S(1)}, bf16[128,4,128]{2,0,1:T(8,128)(2,1)S(1)}, u32[]{:S(2)}, u32[]{:S(2)}) collective-permute-start(bf16[128,4,128]{2,0,1:T(8,128)(2,1)S(1)} %copy.96), channel_id=1, source_target_pairs={{0,4},{1,5},{2,6},{3,7},{4,8},{5,9},{6,10},{7,11},{8,12},{9,13},{1... | collective-permute-start | bytes 393224 | tf_op jit(solution)/shard_map/ppermute | solution.py:12
  35.9 0.8 fusion.11
  36.7 0.6 fusion.45
  37.3 0.0 collective-permute-done.1
  37.3 5.2 %collective-permute-start.4 = (bf16[128,4,128]{2,0,1:T(8,128)(2,1)S(1)}, bf16[128,4,128]{2,0,1:T(8,128)(2,1)S(1)}, u32[]{:S(2)}, u32[]{:S(2)}) collective-permute-start(bf16[128,4,128]{2,0,1:T(8,128)(2,1)S(1)} %copy.96), channel_id=1, source_target_pairs={{0,3},{1,4},{2,5},{3,6},{4,7},{5,8},{6,9},{7,10},{8,11},{9,12},{10... | collective-permute-start | bytes 393224 | tf_op jit(solution)/shard_map/ppermute | solution.py:12
  42.6 0.7 fusion.13
  43.2 0.6 fusion.42
  43.8 5.1 %collective-permute-done.4 = bf16[128,4,128]{2,0,1:T(8,128)(2,1)S(1)} collective-permute-done((bf16[128,4,128]{2,0,1:T(8,128)(2,1)S(1)}, bf16[128,4,128]{2,0,1:T(8,128)(2,1)S(1)}, u32[]{:S(2)}, u32[]{:S(2)}) %collective-permute-start.4) | collective-permute-done | bytes 131104 | tf_op jit(solution)/shard_map/ppermute | solution.py:12
  48.9 1.9 %collective-permute-start.8 = (bf16[128,4,128]{2,0,1:T(8,128)(2,1)S(1)}, bf16[128,4,128]{2,0,1:T(8,128)(2,1)S(1)}, u32[]{:S(2)}, u32[]{:S(2)}) collective-permute-start(bf16[128,4,128]{2,0,1:T(8,128)(2,1)S(1)} %fusion.42), channel_id=1, source_target_pairs={{1,0},{2,1},{3,2},{4,3},{5,4},{6,5},{7,6},{8,7},{9,8},{10,9},{11,1... | collective-permute-start | bytes 393224 | tf_op jit(solution)/shard_map/ppermute | solution.py:12
  50.8 0.8 fusion.7
  51.6 0.6 fusion.44
  52.2 0.0 collective-permute-done.3
  52.2 2.5 %collective-permute-start.12 = (bf16[128,4,128]{2,0,1:T(8,128)(2,1)S(1)}, bf16[128,4,128]{2,0,1:T(8,128)(2,1)S(1)}, u32[]{:S(2)}, u32[]{:S(2)}) collective-permute-start(bf16[128,4,128]{2,0,1:T(8,128)(2,1)S(1)} %fusion.46), channel_id=1, source_target_pairs={{1,0},{2,1},{3,2},{4,3},{5,4},{6,5},{7,6},{8,7},{9,8},{10,9},{11,1... | collective-permute-start | bytes 393224 | tf_op jit(solution)/shard_map/ppermute | solution.py:12
  54.7 0.7 fusion.9
  55.4 0.6 fusion.41
  56.0 6.4 %collective-permute-start.9 = (bf16[128,4,128]{2,0,1:T(8,128)(2,1)S(1)}, bf16[128,4,128]{2,0,1:T(8,128)(2,1)S(1)}, u32[]{:S(2)}, u32[]{:S(2)}) collective-permute-start(bf16[128,4,128]{2,0,1:T(8,128)(2,1)S(1)} %fusion.41), channel_id=1, source_target_pairs={{2,0},{3,1},{4,2},{5,3},{6,4},{7,5},{8,6},{9,7},{10,8},{11,9},{12,... | collective-permute-start | bytes 393224 | tf_op jit(solution)/shard_map/ppermute | solution.py:12
  62.4 0.7 fusion.5
  63.1 0.6 fusion.40
  63.7 2.5 %collective-permute-start.10 = (bf16[128,4,128]{2,0,1:T(8,128)(2,1)S(1)}, bf16[128,4,128]{2,0,1:T(8,128)(2,1)S(1)}, u32[]{:S(2)}, u32[]{:S(2)}) collective-permute-start(bf16[128,4,128]{2,0,1:T(8,128)(2,1)S(1)} %fusion.40), channel_id=1, source_target_pairs={{3,0},{4,1},{5,2},{6,3},{7,4},{8,5},{9,6},{10,7},{11,8},{12,9},{13... | collective-permute-start | bytes 393224 | tf_op jit(solution)/shard_map/ppermute | solution.py:12
  66.2 0.8 fusion.3
  67.0 0.6 fusion.43
  67.6 0.0 collective-permute-done.7
  67.6 0.7 fusion.1
  68.2 0.6 fusion.39
  68.8 2.2 %collective-permute-start.11 = (bf16[128,4,128]{2,0,1:T(8,128)(2,1)S(1)}, bf16[128,4,128]{2,0,1:T(8,128)(2,1)S(1)}, u32[]{:S(2)}, u32[]{:S(2)}) collective-permute-start(bf16[128,4,128]{2,0,1:T(8,128)(2,1)S(1)} %fusion.39), channel_id=1, source_target_pairs={{4,0},{5,1},{6,2},{7,3},{8,4},{9,5},{10,6},{11,7},{12,8},{13,9},{1... | collective-permute-start | bytes 393224 | tf_op jit(solution)/shard_map/ppermute | solution.py:12
  71.1 0.5 fusion.67
  71.6 0.5 fusion.63
  72.1 0.5 fusion.59
  72.7 0.7 multiply_convert_fusion
  73.4 1.6 %copy.126 = bf16[128,32,128]{2,1,0:T(8,128)(2,1)} copy(bf16[128,32,128]{2,0,1:T(8,128)(2,1)S(1)} %bitcast.263) | data formatting | bytes 2097152
  75.1 0.0 collective-permute-done.8
  75.1 1.9 %collective-permute-start.13 = (bf16[128,4,128]{2,0,1:T(8,128)(2,1)S(1)}, bf16[128,4,128]{2,0,1:T(8,128)(2,1)S(1)}, u32[]{:S(2)}, u32[]{:S(2)}) collective-permute-start(bf16[128,4,128]{2,0,1:T(8,128)(2,1)S(1)} %fusion.45), channel_id=1, source_target_pairs={{2,0},{3,1},{4,2},{5,3},{6,4},{7,5},{8,6},{9,7},{10,8},{11,9},{12,... | collective-permute-start | bytes 393224 | tf_op jit(solution)/shard_map/ppermute | solution.py:12
  77.0 3.3 %collective-permute-start.14 = (bf16[128,4,128]{2,0,1:T(8,128)(2,1)S(1)}, bf16[128,4,128]{2,0,1:T(8,128)(2,1)S(1)}, u32[]{:S(2)}, u32[]{:S(2)}) collective-permute-start(bf16[128,4,128]{2,0,1:T(8,128)(2,1)S(1)} %fusion.44), channel_id=1, source_target_pairs={{3,0},{4,1},{5,2},{6,3},{7,4},{8,5},{9,6},{10,7},{11,8},{12,9},{13... | collective-permute-start | bytes 393224 | tf_op jit(solution)/shard_map/ppermute | solution.py:12
  80.3 1.9 %collective-permute-start.15 = (bf16[128,4,128]{2,0,1:T(8,128)(2,1)S(1)}, bf16[128,4,128]{2,0,1:T(8,128)(2,1)S(1)}, u32[]{:S(2)}, u32[]{:S(2)}) collective-permute-start(bf16[128,4,128]{2,0,1:T(8,128)(2,1)S(1)} %fusion.43), channel_id=1, source_target_pairs={{4,0},{5,1},{6,2},{7,3},{8,4},{9,5},{10,6},{11,7},{12,8},{13,9},{1... | collective-permute-start | bytes 393224 | tf_op jit(solution)/shard_map/ppermute | solution.py:12
  82.2 0.0 collective-permute-done.11
  82.3 0.6 add_convert_fusion.1
  82.8 0.8 copy.127
  83.6 5.4 %collective-permute-done.14 = bf16[128,4,128]{2,0,1:T(8,128)(2,1)S(1)} collective-permute-done((bf16[128,4,128]{2,0,1:T(8,128)(2,1)S(1)}, bf16[128,4,128]{2,0,1:T(8,128)(2,1)S(1)}, u32[]{:S(2)}, u32[]{:S(2)}) %collective-permute-start.14) | collective-permute-done | bytes 131104 | tf_op jit(solution)/shard_map/ppermute | solution.py:12
  89.0 5.7 %collective-permute-done.15 = bf16[128,4,128]{2,0,1:T(8,128)(2,1)S(1)} collective-permute-done((bf16[128,4,128]{2,0,1:T(8,128)(2,1)S(1)}, bf16[128,4,128]{2,0,1:T(8,128)(2,1)S(1)}, u32[]{:S(2)}, u32[]{:S(2)}) %collective-permute-start.15) | collective-permute-done | bytes 131104 | tf_op jit(solution)/shard_map/ppermute | solution.py:12
  94.7 0.6 add_convert_fusion
  95.2 0.8 copy.128
  (17 shorter events, 0.1 us)
Async XLA Ops:
  0.6 24.3 %copy-start = (bf16[128,32,128]{2,1,0:T(8,128)(2,1)S(1)}, bf16[128,32,128]{2,1,0:T(8,128)(2,1)}, u32[]{:S(2)}) copy-start(bf16[128,32,128]{2,1,0:T(8,128)(2,1)} %param.7) | copy-start | bytes 3145732
  0.6 24.3 %copy-start.3 = (bf16[128,4,128]{2,1,0:T(4,128)(2,1)S(1)}, bf16[128,4,128]{2,1,0:T(4,128)(2,1)}, u32[]{:S(2)}) copy-start(bf16[128,4,128]{2,1,0:T(4,128)(2,1)} %param.8) | copy-start | bytes 393220
  0.7 24.2 %copy-start.4 = (f32[32,128]{1,0:T(8,128)S(1)}, f32[32,128]{1,0:T(8,128)}, u32[]{:S(2)}) copy-start(f32[32,128]{1,0:T(8,128)} %param.12) | copy-start | bytes 49156
  1.7 65.9 %collective-permute-start.7 = (bf16[128,4,128]{2,0,1:T(8,128)(2,1)S(1)}, bf16[128,4,128]{2,0,1:T(8,128)(2,1)S(1)}, u32[]{:S(2)}, u32[]{:S(2)}) collective-permute-start(bf16[128,4,128]{2,0,1:T(8,128)(2,1)S(1)} %copy.98), channel_id=1, source_target_pairs={{0,4},{1,5},{2,6},{3,7},{4,8},{5,9},{6,10},{7,11},{8,12},{9,13},{1... | collective-permute-start | bytes 393224 | tf_op jit(solution)/shard_map/ppermute | solution.py:12
  6.6 49.4 %collective-permute-start.5 = (bf16[128,4,128]{2,0,1:T(8,128)(2,1)S(1)}, bf16[128,4,128]{2,0,1:T(8,128)(2,1)S(1)}, u32[]{:S(2)}, u32[]{:S(2)}) collective-permute-start(bf16[128,4,128]{2,0,1:T(8,128)(2,1)S(1)} %copy.98), channel_id=1, source_target_pairs={{0,3},{1,4},{2,5},{3,6},{4,7},{5,8},{6,9},{7,10},{8,11},{9,12},{10... | collective-permute-start | bytes 393224 | tf_op jit(solution)/shard_map/ppermute | solution.py:12
  12.7 39.6 %collective-permute-start.3 = (bf16[128,4,128]{2,0,1:T(8,128)(2,1)S(1)}, bf16[128,4,128]{2,0,1:T(8,128)(2,1)S(1)}, u32[]{:S(2)}, u32[]{:S(2)}) collective-permute-start(bf16[128,4,128]{2,0,1:T(8,128)(2,1)S(1)} %copy.98), channel_id=1, source_target_pairs={{0,2},{1,3},{2,4},{3,5},{4,6},{5,7},{6,8},{7,9},{8,10},{9,11},{10,... | collective-permute-start | bytes 393224 | tf_op jit(solution)/shard_map/ppermute | solution.py:12
  15.3 22.0 %collective-permute-start.1 = (bf16[128,4,128]{2,0,1:T(8,128)(2,1)S(1)}, bf16[128,4,128]{2,0,1:T(8,128)(2,1)S(1)}, u32[]{:S(2)}, u32[]{:S(2)}) collective-permute-start(bf16[128,4,128]{2,0,1:T(8,128)(2,1)S(1)} %copy.98), channel_id=1, source_target_pairs={{0,1},{1,2},{2,3},{3,4},{4,5},{5,6},{6,7},{7,8},{8,9},{9,10},{10,1... | collective-permute-start | bytes 393224 | tf_op jit(solution)/shard_map/ppermute | solution.py:12
  18.2 8.7 %collective-permute-start = (bf16[128,4,128]{2,0,1:T(8,128)(2,1)S(1)}, bf16[128,4,128]{2,0,1:T(8,128)(2,1)S(1)}, u32[]{:S(2)}, u32[]{:S(2)}) collective-permute-start(bf16[128,4,128]{2,0,1:T(8,128)(2,1)S(1)} %copy.96), channel_id=1, source_target_pairs={{0,1},{1,2},{2,3},{3,4},{4,5},{5,6},{6,7},{7,8},{8,9},{9,10},{10,1... | collective-permute-start | bytes 393224 | tf_op jit(solution)/shard_map/ppermute | solution.py:12
  23.5 2.3 %copy-start.1 = (bf16[128,32,128]{2,1,0:T(8,128)(2,1)S(1)}, bf16[128,32,128]{2,1,0:T(8,128)(2,1)}, u32[]{:S(2)}) copy-start(bf16[128,32,128]{2,1,0:T(8,128)(2,1)} %param.11) | copy-start | bytes 3145732
  23.5 2.3 %copy-start.2 = (bf16[128,4,128]{2,1,0:T(4,128)(2,1)S(1)}, bf16[128,4,128]{2,1,0:T(4,128)(2,1)}, u32[]{:S(2)}) copy-start(bf16[128,4,128]{2,1,0:T(4,128)(2,1)} %param.9) | copy-start | bytes 393220
  26.9 7.1 %collective-permute-start.2 = (bf16[128,4,128]{2,0,1:T(8,128)(2,1)S(1)}, bf16[128,4,128]{2,0,1:T(8,128)(2,1)S(1)}, u32[]{:S(2)}, u32[]{:S(2)}) collective-permute-start(bf16[128,4,128]{2,0,1:T(8,128)(2,1)S(1)} %copy.96), channel_id=1, source_target_pairs={{0,2},{1,3},{2,4},{3,5},{4,6},{5,7},{6,8},{7,9},{8,10},{9,11},{10,... | collective-permute-start | bytes 393224 | tf_op jit(solution)/shard_map/ppermute | solution.py:12
  34.0 29.6 %collective-permute-start.6 = (bf16[128,4,128]{2,0,1:T(8,128)(2,1)S(1)}, bf16[128,4,128]{2,0,1:T(8,128)(2,1)S(1)}, u32[]{:S(2)}, u32[]{:S(2)}) collective-permute-start(bf16[128,4,128]{2,0,1:T(8,128)(2,1)S(1)} %copy.96), channel_id=1, source_target_pairs={{0,4},{1,5},{2,6},{3,7},{4,8},{5,9},{6,10},{7,11},{8,12},{9,13},{1... | collective-permute-start | bytes 393224 | tf_op jit(solution)/shard_map/ppermute | solution.py:12
  37.3 11.6 %collective-permute-start.4 = (bf16[128,4,128]{2,0,1:T(8,128)(2,1)S(1)}, bf16[128,4,128]{2,0,1:T(8,128)(2,1)S(1)}, u32[]{:S(2)}, u32[]{:S(2)}) collective-permute-start(bf16[128,4,128]{2,0,1:T(8,128)(2,1)S(1)} %copy.96), channel_id=1, source_target_pairs={{0,3},{1,4},{2,5},{3,6},{4,7},{5,8},{6,9},{7,10},{8,11},{9,12},{10... | collective-permute-start | bytes 393224 | tf_op jit(solution)/shard_map/ppermute | solution.py:12
  48.9 26.2 %collective-permute-start.8 = (bf16[128,4,128]{2,0,1:T(8,128)(2,1)S(1)}, bf16[128,4,128]{2,0,1:T(8,128)(2,1)S(1)}, u32[]{:S(2)}, u32[]{:S(2)}) collective-permute-start(bf16[128,4,128]{2,0,1:T(8,128)(2,1)S(1)} %fusion.42), channel_id=1, source_target_pairs={{1,0},{2,1},{3,2},{4,3},{5,4},{6,5},{7,6},{8,7},{9,8},{10,9},{11,1... | collective-permute-start | bytes 393224 | tf_op jit(solution)/shard_map/ppermute | solution.py:12
  52.2 31.4 %collective-permute-start.12 = (bf16[128,4,128]{2,0,1:T(8,128)(2,1)S(1)}, bf16[128,4,128]{2,0,1:T(8,128)(2,1)S(1)}, u32[]{:S(2)}, u32[]{:S(2)}) collective-permute-start(bf16[128,4,128]{2,0,1:T(8,128)(2,1)S(1)} %fusion.46), channel_id=1, source_target_pairs={{1,0},{2,1},{3,2},{4,3},{5,4},{6,5},{7,6},{8,7},{9,8},{10,9},{11,1... | collective-permute-start | bytes 393224 | tf_op jit(solution)/shard_map/ppermute | solution.py:12
  56.0 21.0 %collective-permute-start.9 = (bf16[128,4,128]{2,0,1:T(8,128)(2,1)S(1)}, bf16[128,4,128]{2,0,1:T(8,128)(2,1)S(1)}, u32[]{:S(2)}, u32[]{:S(2)}) collective-permute-start(bf16[128,4,128]{2,0,1:T(8,128)(2,1)S(1)} %fusion.41), channel_id=1, source_target_pairs={{2,0},{3,1},{4,2},{5,3},{6,4},{7,5},{8,6},{9,7},{10,8},{11,9},{12,... | collective-permute-start | bytes 393224 | tf_op jit(solution)/shard_map/ppermute | solution.py:12
  63.7 16.6 %collective-permute-start.10 = (bf16[128,4,128]{2,0,1:T(8,128)(2,1)S(1)}, bf16[128,4,128]{2,0,1:T(8,128)(2,1)S(1)}, u32[]{:S(2)}, u32[]{:S(2)}) collective-permute-start(bf16[128,4,128]{2,0,1:T(8,128)(2,1)S(1)} %fusion.40), channel_id=1, source_target_pairs={{3,0},{4,1},{5,2},{6,3},{7,4},{8,5},{9,6},{10,7},{11,8},{12,9},{13... | collective-permute-start | bytes 393224 | tf_op jit(solution)/shard_map/ppermute | solution.py:12
  68.8 13.4 %collective-permute-start.11 = (bf16[128,4,128]{2,0,1:T(8,128)(2,1)S(1)}, bf16[128,4,128]{2,0,1:T(8,128)(2,1)S(1)}, u32[]{:S(2)}, u32[]{:S(2)}) collective-permute-start(bf16[128,4,128]{2,0,1:T(8,128)(2,1)S(1)} %fusion.39), channel_id=1, source_target_pairs={{4,0},{5,1},{6,2},{7,3},{8,4},{9,5},{10,6},{11,7},{12,8},{13,9},{1... | collective-permute-start | bytes 393224 | tf_op jit(solution)/shard_map/ppermute | solution.py:12
  75.1 8.5 %collective-permute-start.13 = (bf16[128,4,128]{2,0,1:T(8,128)(2,1)S(1)}, bf16[128,4,128]{2,0,1:T(8,128)(2,1)S(1)}, u32[]{:S(2)}, u32[]{:S(2)}) collective-permute-start(bf16[128,4,128]{2,0,1:T(8,128)(2,1)S(1)} %fusion.45), channel_id=1, source_target_pairs={{2,0},{3,1},{4,2},{5,3},{6,4},{7,5},{8,6},{9,7},{10,8},{11,9},{12,... | collective-permute-start | bytes 393224 | tf_op jit(solution)/shard_map/ppermute | solution.py:12
  77.0 12.0 %collective-permute-start.14 = (bf16[128,4,128]{2,0,1:T(8,128)(2,1)S(1)}, bf16[128,4,128]{2,0,1:T(8,128)(2,1)S(1)}, u32[]{:S(2)}, u32[]{:S(2)}) collective-permute-start(bf16[128,4,128]{2,0,1:T(8,128)(2,1)S(1)} %fusion.44), channel_id=1, source_target_pairs={{3,0},{4,1},{5,2},{6,3},{7,4},{8,5},{9,6},{10,7},{11,8},{12,9},{13... | collective-permute-start | bytes 393224 | tf_op jit(solution)/shard_map/ppermute | solution.py:12
  80.3 14.4 %collective-permute-start.15 = (bf16[128,4,128]{2,0,1:T(8,128)(2,1)S(1)}, bf16[128,4,128]{2,0,1:T(8,128)(2,1)S(1)}, u32[]{:S(2)}, u32[]{:S(2)}) collective-permute-start(bf16[128,4,128]{2,0,1:T(8,128)(2,1)S(1)} %fusion.43), channel_id=1, source_target_pairs={{4,0},{5,1},{6,2},{7,3},{8,4},{9,5},{10,6},{11,7},{12,8},{13,9},{1... | collective-permute-start | bytes 393224 | tf_op jit(solution)/shard_map/ppermute | solution.py:12
where the time goes:
time: 96.6 us; the launch traced here: 96 us
  starting transfers between devices  50.2 us (52%)
  waiting for transfers between devices  19.9 us (21%)
  matrix products  15.9 us (16%)
  local copies, waits for them, and re-layouts  5.2 us (5%)
  other arithmetic  3.53 us (4%)
  between operations  1.17 us (1%)
    ppermute x16, starting transfers between devices, from_behind(): lax.ppermute(value, axis, [(source, source + steps) for source in range(i...  50.2 us
    ppermute x16, waiting for transfers between devices, from_behind(): lax.ppermute(value, axis, [(source, source + steps) for source in range(i...  19.9 us
    unnamed x15, local copies, waits for them, and re-layouts  5.14 us
    dot_general x5, matrix products, gradients(): jnp.einsum('tkgd,skd->kgts', query_grp, key_blk, preferred_element_type=j...  3.93 us
    dot_general x5, matrix products, gradients(): jnp.einsum('tkgd,skd->kgts', grad_grp, val_blk, preferred_element_type=jn...  3.27 us
    dot_general x5, matrix products, gradients(): jnp.einsum('kgts,tkgd->skd', probs_low, grad_grp, preferred_element_type=...  2.95 us
    dot_general x5, matrix products, gradients(): jnp.einsum('kgts,tkgd->skd', dscores, query_grp, preferred_element_type=j...  2.91 us
    dot_general x5, matrix products, gradients(): jnp.einsum('kgts,skd->tkgd', dscores, key_blk, preferred_element_type=jnp...  2.88 us
  transfers between devices with their start and end apart: 16, of which 4 were waited for; matrix products, arithmetic and copies ran while one was open for 23% of the time, Pallas kernels for 0%

commit v1 on v0

v1 whole, which is shorter than its diff:
```python
import functools

import jax
import jax.numpy as jnp
from jax import lax
from jax.experimental import pallas as pl
from jax.experimental.pallas import tpu as pltpu
from jax.sharding import PartitionSpec as P

F32 = jnp.float32
BF16 = jnp.bfloat16
MESH = pl.DeviceIdType.MESH
NT = (((1,), (1,)), ((), ()))
NN = (((1,), (0,)), ((), ()))
TN = (((0,), (0,)), ((), ()))
LOG2E = 1.4426950408889634


def dot(a, b, dims):
    return lax.dot_general(a, b, dims, preferred_element_type=F32)


def kernel(n_chips, width, group, scale,
           q_hbm, k_hbm, v_hbm, o_hbm, g_hbm, lse_hbm, doc_hbm,
           dq_out, dk_out, dv_out,
           qs, gs, os_, lse_in, docs, kin, vin, own_kv, kvb, bias, lse_b, dl_b, dq_acc, dq_send,
           parts, d0, ret, rb0, rb1, rb2,
           loc_sem, xs, xr, ks, kr0, kr1, fs, fr, rs0, rs1, rs2, rr0, rr1, rr2, dqs, dqr):
    me = lax.axis_index("seq")
    core = lax.rem(me, 2)
    chip = me // 2
    other = 1 - core
    rows = width * group

    def device(step, which):
        return {"seq": lax.rem(chip + step + n_chips, n_chips) * 2 + which}

    sibling = device(0, other)

    barrier = pltpu.get_barrier_semaphore()
    pl.semaphore_signal(barrier, inc=1, device_id=sibling, device_id_type=MESH)
    pl.semaphore_signal(barrier, inc=1, device_id=device(-1, 0), device_id_type=MESH)
    pl.semaphore_signal(barrier, inc=1, device_id=device(-1, 1), device_id_type=MESH)

    def remote(src, dst, send, recv, to):
        return pltpu.make_async_remote_copy(
            src_ref=src, dst_ref=dst, send_sem=send, recv_sem=recv, device_id=to, device_id_type=MESH
        )

    local = [
        pltpu.make_async_copy(k_hbm, kin, loc_sem.at[0]),
        pltpu.make_async_copy(v_hbm, vin, loc_sem.at[1]),
        pltpu.make_async_copy(doc_hbm, docs, loc_sem.at[2]),
        pltpu.make_async_copy(lse_hbm.at[pl.ds(2 * core, 2)], lse_in.at[:, core], loc_sem.at[3]),
    ]
    for j in range(2):
        for i, (src, dst) in enumerate(((q_hbm, qs), (g_hbm, gs), (o_hbm, os_))):
            local.append(
                pltpu.make_async_copy(src.at[:, 2 * core + j], dst.at[j, core], loc_sem.at[4 + 3 * j + i])
            )
    for copy in local:
        copy.start()

    local[0].wait()
    local[1].wait()
    own_kv[:, 0] = jnp.transpose(kin[...], (1, 0, 2))
    own_kv[:, 1] = jnp.transpose(vin[...], (1, 0, 2))
    for j in range(2):
        kvb[0, j, core] = own_kv[2 * core + j]

    local[2].wait()

    def mask_step(index, carry):
        back = index // 4
        key_half = lax.rem(index // 2, 2)
        query_half = lax.rem(index, 2)
        key_chip = chip - back
        key_row = lax.rem(key_chip + n_chips, n_chips) * 2 + key_half
        query_row = chip * 2 + query_half
        key_doc = docs[pl.ds(key_row, 1), :].astype(F32)
        query_doc = docs[pl.ds(query_row, 1), :].astype(F32)
        query_col = jnp.broadcast_to(query_doc, (width, width)).T
        t = lax.broadcasted_iota(jnp.int32, (width, width), 0) + query_row * width
        p = lax.broadcasted_iota(jnp.int32, (width, width), 1) + (key_chip * 2 + key_half) * width
        live = (query_col == key_doc) & (p <= t) & (p >= 0)
        block = jnp.where(live, 0.0, -jnp.inf).astype(F32)
        wide = jnp.broadcast_to(block[:, None, :], (width, group, width)).reshape(rows, width)
        bias[back, key_half, pl.ds(pl.multiple_of(query_half * rows, rows), rows), :] = wide
        return carry

    lax.fori_loop(0, 12, mask_step, 0)

    def row_terms(j, half):
        start = pl.multiple_of(half * rows, rows)
        row = lse_in[j, half] * LOG2E
        lse_b[j, pl.ds(start, rows), :] = jnp.broadcast_to(row.T[:, :, None], (width, group, 128)).reshape(rows, 128)
        g = gs[j, half].reshape(rows, 128).astype(F32)
        o = os_[j, half].reshape(rows, 128).astype(F32)
        dl_b[j, pl.ds(start, rows), :] = jnp.broadcast_to(jnp.sum(g * o, axis=-1, keepdims=True), (rows, 128))

    def block(j, back, key_half, half, halves, first):
        start = pl.multiple_of(half * rows, rows)
        count = rows * halves
        r = pl.ds(start, count)
        if halves == 1:
            q = qs[j, half].reshape(count, 128)
            g = gs[j, half].reshape(count, 128)
        else:
            q = qs[j].reshape(count, 128)
            g = gs[j].reshape(count, 128)
        k = kvb[back, j, key_half, 0]
        v = kvb[back, j, key_half, 1]
        s = dot(q, k, NT)
        dp = dot(g, v, NT)
        p = jnp.exp2(s * (scale * LOG2E) - lse_b[j, r, :] + bias[back, key_half, r, :])
        ds = (p * (dp - dl_b[j, r, :])).astype(BF16)
        p = p.astype(BF16)
        term = dot(ds, k, NN)
        if first:
            dq_acc[j, r, :] = term
        else:
            dq_acc[j, r, :] += term
        return dot(q, ds, TN) * scale, dot(g, p, TN)

    for copy in local[3:]:
        copy.wait()

    def own_step(j, carry):
        row_terms(j, core)
        dk, dv = block(j, 0, core, core, 1, True)
        parts[0, j, 0] = dk
        parts[0, j, 1] = dv
        return carry

    lax.fori_loop(0, 2, own_step, 0)

    pl.semaphore_wait(barrier, 3)

    sends = []
    for j in range(2):
        for x, which in enumerate((core, other)):
            sends.append(
                remote(own_kv.at[2 * which + j], kvb.at[1, j, core], ks.at[2 * j + x], kr1.at[j, core], device(1, which))
            )
    for copy in sends:
        copy.start()
    swaps = [
        remote(lse_hbm.at[pl.ds(2 * other, 2)], lse_in.at[:, core], xs.at[6], xr.at[6], sibling),
    ]
    for j in range(2):
        for i, (src, dst) in enumerate(((g_hbm, gs), (o_hbm, os_), (q_hbm, qs))):
            swaps.append(remote(src.at[:, 2 * other + j], dst.at[j, core], xs.at[3 * j + i], xr.at[3 * j + i], sibling))
        swaps.append(remote(own_kv.at[2 * other + j], kvb.at[0, j, core], ks.at[4 + j], kr0.at[j], sibling))
    for copy in swaps:
        copy.start()

    def arrival(dst, sem):
        return remote(dst, dst, fs.at[0], sem, sibling)

    arrival(lse_in.at[:, other], xr.at[6]).wait_recv()

    def sibling_step(j, carry):
        for i, dst in enumerate((gs, os_, qs)):
            arrival(dst.at[j, other], xr.at[3 * j + i]).wait_recv()
        row_terms(j, other)
        arrival(kvb.at[0, j, other], kr0.at[j]).wait_recv()
        dk, dv = block(j, 0, other, other, 1, True)
        parts[1, j, 0] = dk
        parts[1, j, 1] = dv
        dk, dv = block(j, 0, 0, 1, 1, False)
        parts[core, j, 0] += dk
        parts[core, j, 1] += dv
        ret[j] = parts[1, j].astype(BF16)
        remote(ret.at[j], rb0.at[j], rs0.at[j], rr0.at[j], sibling).start()
        return carry

    lax.fori_loop(0, 2, sibling_step, 0)

    def near_step(n, carry):
        j = n // 2
        a = jnp.where(lax.rem(n, 2) == 0, core, other)
        arrival(kvb.at[1, j, a], kr1.at[j, a]).wait_recv()
        remote(kvb.at[1, j, a], kvb.at[2, j, a], fs.at[n], fr.at[j, a], device(1, core)).start()
        dk, dv = block(j, 1, a, 0, 2, False)
        ret[2 + n, 0] = dk.astype(BF16)
        ret[2 + n, 1] = dv.astype(BF16)
        remote(ret.at[2 + n], rb1.at[2 * core + j], rs1.at[n], rr1.at[2 * core + j], device(-1, a)).start()
        return carry

    lax.fori_loop(0, 4, near_step, 0)

    def far_step(n, carry):
        j = n // 2
        a = jnp.where(lax.rem(n, 2) == 0, core, other)
        arrival(kvb.at[2, j, a], fr.at[j, a]).wait_recv()
        dk, dv = block(j, 2, a, 0, 1, False)
        ret[6 + n, 0] = dk.astype(BF16)
        ret[6 + n, 1] = dv.astype(BF16)

        @pl.when(a == 1)
        def _():
            dk2, dv2 = block(j, 2, a, 1, 1, False)
            ret[6 + n, 0] = (dk + dk2).astype(BF16)
            ret[6 + n, 1] = (dv + dv2).astype(BF16)

        remote(ret.at[6 + n], rb2.at[2 * core + j], rs2.at[n], rr2.at[2 * core + j], device(-2, a)).start()

        @pl.when(lax.rem(n, 2) == 1)
        def _():
            mine = dq_acc[j, pl.ds(pl.multiple_of(core * rows, rows), rows), :] * scale
            theirs = dq_acc[j, pl.ds(pl.multiple_of(other * rows, rows), rows), :] * scale
            dq_send[j] = theirs.astype(BF16).reshape(width, group, 128)
            remote(dq_send.at[j], dq_out.at[:, 2 * core + j], dqs.at[j], dqr.at[j], sibling).start()
            dq_out[:, 2 * core + j] = mine.astype(BF16).reshape(width, group, 128)

        return carry

    lax.fori_loop(0, 4, far_step, 0)

    for j in range(2):
        arrival(rb0.at[j], rr0.at[j]).wait_recv()
        d0[2 * core + j] = parts[0, j]
        d0[2 * other + j] = rb0[j].astype(F32)
    for h in range(4):
        arrival(rb1.at[h], rr1.at[h]).wait_recv()
    for h in range(4):
        arrival(rb2.at[h], rr2.at[h]).wait_recv()
    for i, out in enumerate((dk_out, dv_out)):
        heads = [(d0[h, i] + rb1[h, i].astype(F32) + rb2[h, i].astype(F32)).T for h in range(4)]
        out[...] = jnp.transpose(jnp.stack(heads), (1, 0, 2)).astype(BF16)

    for j in range(2):
        remote(dq_send.at[j], dq_out.at[:, 2 * other + j], dqs.at[j], dqr.at[j], sibling).wait()
        remote(ret.at[j], rb0.at[j], rs0.at[j], rr0.at[j], sibling).wait_send()
    for copy in sends + swaps:
        copy.wait_send()
    for n in range(4):
        remote(kvb.at[1, 0, 0], kvb.at[2, 0, 0], fs.at[n], fr.at[0, 0], sibling).wait_send()
        remote(ret.at[2 + n], rb1.at[0], rs1.at[n], rr1.at[0], sibling).wait_send()
        remote(ret.at[6 + n], rb2.at[0], rs2.at[n], rr2.at[0], sibling).wait_send()


def on_device(n_chips, queries, keys, values, attn_out, out_grad, log_sums, doc_ids):
    width, heads, size = queries.shape
    kv = keys.shape[1]
    group = heads // kv
    rows = width * group
    split = (width, kv, group, size)
    any_spec = pl.BlockSpec(memory_space=pl.ANY)
    vmem_spec = pl.BlockSpec(memory_space=pltpu.VMEM)
    dma = pltpu.SemaphoreType.DMA
    dq, dk, dv = pl.pallas_call(
        functools.partial(kernel, n_chips, width, group, size ** -0.5),
        out_shape=(
            jax.ShapeDtypeStruct(split, BF16),
            jax.ShapeDtypeStruct(keys.shape, BF16),
            jax.ShapeDtypeStruct(keys.shape, BF16),
        ),
        in_specs=[any_spec] * 7,
        out_specs=(vmem_spec,) * 3,
        scratch_shapes=[
            pltpu.VMEM((2, 2, width, group, size), BF16),
            pltpu.VMEM((2, 2, width, group, size), BF16),
            pltpu.VMEM((2, 2, width, group, size), BF16),
            pltpu.VMEM((2, 2, group, width), F32),
            pltpu.VMEM((2 * n_chips, width), jnp.int32),
            pltpu.VMEM(keys.shape, BF16),
            pltpu.VMEM(keys.shape, BF16),
            pltpu.VMEM((kv, 2, width, size), BF16),
            pltpu.VMEM((3, 2, 2, 2, width, size), BF16),
            pltpu.VMEM((3, 2, 2 * rows, width), F32),
            pltpu.VMEM((2, 2 * rows, 128), F32),
            pltpu.VMEM((2, 2 * rows, 128), F32),
            pltpu.VMEM((2, 2 * rows, size), F32),
            pltpu.VMEM((2, width, group, size), BF16),
            pltpu.VMEM((2, 2, 2, size, width), F32),
            pltpu.VMEM((kv, 2, size, width), F32),
            pltpu.VMEM((10, 2, size, width), BF16),
            pltpu.VMEM((2, 2, size, width), BF16),
            pltpu.VMEM((kv, 2, size, width), BF16),
            pltpu.VMEM((kv, 2, size, width), BF16),
            dma((10,)), dma((7,)), dma((7,)), dma((6,)), dma((2,)), dma((2, 2)), dma((4,)), dma((2, 2)),
            dma((2,)), dma((4,)), dma((4,)), dma((2,)), dma((4,)), dma((4,)), dma((2,)), dma((2,)),
        ],
        compiler_params=pltpu.CompilerParams(
            collective_id=0, has_side_effects=True, vmem_limit_bytes=60 * 2**20
        ),
    )(
        queries.reshape(split), keys, values, attn_out.reshape(split), out_grad.reshape(split),
        log_sums.reshape(kv, group, width), doc_ids.reshape(2 * n_chips, width),
    )
    return dq.reshape(queries.shape), dk, dv


def solution(mesh):
    placed = (
        P(("dp", "seq"), None, None),
        P(("dp", "seq"), None, None),
        P(("dp", "seq"), None, None),
        P(("dp", "seq"), None, None),
        P(("dp", "seq"), None, None),
        P(None, ("dp", "seq")),
        P("dp"),
    )
    return jax.shard_map(
        functools.partial(on_device, mesh.shape["seq"] // 2),
        mesh=mesh,
        in_specs=placed,
        out_specs=(P(("dp", "seq"), None, None),) * 3,
        check_vma=False,
    )
```

time: 96.6 us -> 42.4 us (0.44)
  the two profiles are of different devices: /device:TPU:47 before, /device:TPU:1 now
where the time goes in v1:
time: 42.4 us; the launch traced here: 42.3 us
  Pallas kernels  37.7 us (89%)
  local copies, waits for them, and re-layouts  3.91 us (9%)
  between operations  0.65 us (2%)
    pallas_call x1, Pallas kernels, on_device(): pl.pallas_call(functools.partial(kernel, n_chips, width, group, size ** (...  37.7 us
    unnamed x7, local copies, waits for them, and re-layouts  3.91 us

profile of v1, /device:TPU:1, one launch (start us, length us, event | category | flops | bytes accessed | tf_op | source)
XLA Modules:
  0.0 42.3 jit_solution(6378820641626937752)
XLA Ops:
  0.6 37.7 %shard_map.94 = (bf16[128,4,8,128]{3,2,1,0:T(8,128)(2,1)}, bf16[128,4,128]{2,1,0:T(4,128)(2,1)}, bf16[128,4,128]{2,1,0:T(4,128)(2,1)}) custom-call(bf16[128,4,8,128]{3,2,1,0:T(8,128)(2,1)} %bitcast.6, bf16[128,4,128]{2,1,0:T(4,128)(2,1)} %k_hbm.1, bf16[128,4,128]{2,1,0:T(4,128)(2,1)} %v_hbm.1, bf16[128,4,8,128]{3,2,1,0:T(8,128)(2,1)} %bitcast.7, ...), custom_call_target="tpu_custom_call" | custom-call | tf_op jit(solution)/shard_map/pallas_call | solution.py:252
  38.3 0.0 copy-start.1
  38.4 2.3 %copy.13 = bf16[128,32,128]{2,1,0:T(8,128)(2,1)} copy(bf16[128,32,128]{2,1,0:T(8,128)(2,1)} %bitcast.9) | data formatting | bytes 2097152
  40.7 0.0 copy-done.1
  40.7 0.0 copy-start
  40.7 0.7 %copy.14 = bf16[128,4,128]{2,1,0:T(4,128)(2,1)} copy(bf16[128,4,128]{2,1,0:T(4,128)(2,1)S(1)} %copy-done.1) | data formatting | bytes 262144
  41.3 0.3 copy-done
  41.6 0.7 %copy.15 = bf16[128,4,128]{2,1,0:T(4,128)(2,1)} copy(bf16[128,4,128]{2,1,0:T(4,128)(2,1)S(1)} %copy-done) | data formatting | bytes 262144
Async XLA Ops:
  38.3 2.3 %copy-start.1 = (bf16[128,4,128]{2,1,0:T(4,128)(2,1)S(1)}, bf16[128,4,128]{2,1,0:T(4,128)(2,1)}, u32[]{:S(2)}) copy-start(bf16[128,4,128]{2,1,0:T(4,128)(2,1)} %get-tuple-element.13) | copy-start | bytes 393220
  40.7 1.0 %copy-start = (bf16[128,4,128]{2,1,0:T(4,128)(2,1)S(1)}, bf16[128,4,128]{2,1,0:T(4,128)(2,1)}, u32[]{:S(2)}) copy-start(bf16[128,4,128]{2,1,0:T(4,128)(2,1)} %get-tuple-element.14) | copy-start | bytes 393220

commit v2 on v1

--- a/solution.py
+++ b/solution.py
@@ -67,6 +67,26 @@
     own_kv[:, 1] = jnp.transpose(vin[...], (1, 0, 2))
     for j in range(2):
         kvb[0, j, core] = own_kv[2 * core + j]
+
+    pl.semaphore_wait(barrier, 3)
+
+    sends = []
+    for j in range(2):
+        for x, which in enumerate((core, other)):
+            sends.append(
+                remote(own_kv.at[2 * which + j], kvb.at[1, j, core], ks.at[2 * j + x], kr1.at[j, core], device(1, which))
+            )
+    for copy in sends:
+        copy.start()
+    swaps = [
+        remote(lse_hbm.at[pl.ds(2 * other, 2)], lse_in.at[:, core], xs.at[6], xr.at[6], sibling),
+    ]
+    for j in range(2):
+        for i, (src, dst) in enumerate(((g_hbm, gs), (o_hbm, os_), (q_hbm, qs))):
+            swaps.append(remote(src.at[:, 2 * other + j], dst.at[j, core], xs.at[3 * j + i], xr.at[3 * j + i], sibling))
+        swaps.append(remote(own_kv.at[2 * other + j], kvb.at[0, j, core], ks.at[4 + j], kr0.at[j], sibling))
+    for copy in swaps:
+        copy.start()
 
     local[2].wait()
 
@@ -134,26 +154,6 @@
 
     lax.fori_loop(0, 2, own_step, 0)
 
-    pl.semaphore_wait(barrier, 3)
-
-    sends = []
-    for j in range(2):
-        for x, which in enumerate((core, other)):
-            sends.append(
-                remote(own_kv.at[2 * which + j], kvb.at[1, j, core], ks.at[2 * j + x], kr1.at[j, core], device(1, which))
-            )
-    for copy in sends:
-        copy.start()
-    swaps = [
-        remote(lse_hbm.at[pl.ds(2 * other, 2)], lse_in.at[:, core], xs.at[6], xr.at[6], sibling),
-    ]
-    for j in range(2):
-        for i, (src, dst) in enumerate(((g_hbm, gs), (o_hbm, os_), (q_hbm, qs))):
-            swaps.append(remote(src.at[:, 2 * other + j], dst.at[j, core], xs.at[3 * j + i], xr.at[3 * j + i], sibling))
-        swaps.append(remote(own_kv.at[2 * other + j], kvb.at[0, j, core], ks.at[4 + j], kr0.at[j], sibling))
-    for copy in swaps:
-        copy.start()
-
     def arrival(dst, sem):
         return remote(dst, dst, fs.at[0], sem, sibling)
 
@@ -240,6 +240,15 @@
         remote(ret.at[6 + n], rb2.at[0], rs2.at[n], rr2.at[0], sibling).wait_send()
 
 
+def hand_over(*refs):
+    sems = refs[6]
+    copies = [pltpu.make_async_copy(refs[i], refs[3 + i], sems.at[i]) for i in range(3)]
+    for copy in copies:
+        copy.start()
+    for copy in copies:
+        copy.wait()
+
+
 def on_device(n_chips, queries, keys, values, attn_out, out_grad, log_sums, doc_ids):
     width, heads, size = queries.shape
     kv = keys.shape[1]
@@ -252,9 +261,9 @@
     dq, dk, dv = pl.pallas_call(
         functools.partial(kernel, n_chips, width, group, size ** -0.5),
         out_shape=(
-            jax.ShapeDtypeStruct(split, BF16),
-            jax.ShapeDtypeStruct(keys.shape, BF16),
-            jax.ShapeDtypeStruct(keys.shape, BF16),
+            pltpu.VMEM(split, BF16),
+            pltpu.VMEM(keys.shape, BF16),
+            pltpu.VMEM(keys.shape, BF16),
         ),
         in_specs=[any_spec] * 7,
         out_specs=(vmem_spec,) * 3,
@@ -283,12 +292,20 @@
             dma((2,)), dma((4,)), dma((4,)), dma((2,)), dma((4,)), dma((4,)), dma((2,)), dma((2,)),
         ],
         compiler_params=pltpu.CompilerParams(
-            collective_id=0, has_side_effects=True, vmem_limit_bytes=60 * 2**20
+            collective_id=0, has_side_effects=True, vmem_limit_bytes=56 * 2**20
         ),
     )(
         queries.reshape(split), keys, values, attn_out.reshape(split), out_grad.reshape(split),
         log_sums.reshape(kv, group, width), doc_ids.reshape(2 * n_chips, width),
     )
+    dq, dk, dv = pl.pallas_call(
+        hand_over,
+        out_shape=tuple(jax.ShapeDtypeStruct(x.shape, x.dtype) for x in (dq, dk, dv)),
+        in_specs=[vmem_spec] * 3,
+        out_specs=(any_spec,) * 3,
+        scratch_shapes=[dma((3,))],
+        compiler_params=pltpu.CompilerParams(vmem_limit_bytes=2**20),
+    )(dq, dk, dv)
     return dq.reshape(queries.shape), dk, dv
 
 

time: 42.4 us -> 34.9 us (0.82)
  local copies, waits for them, and re-layouts: 3.91 us -> 0 us
  Pallas kernels: 37.7 us -> 33.8 us
    pallas_call x1, Pallas kernels: 37.7 us -> 32.7 us  [on_device(): pl.pallas_call(functools.partial(kernel, n_chips, width, group, size ** (...]
    unnamed x7 -> x0, local copies, waits for them, and re-layouts: 3.91 us -> none
    pallas_call x0 -> x1, Pallas kernels: none -> 1.07 us  [on_device(): pl.pallas_call(hand_over, out_shape=tuple((jax.ShapeDtypeStruct(x.shape,...]
where the time goes in v2:
time: 34.9 us; the launch traced here: 34.4 us
  Pallas kernels  33.8 us (97%)
  between operations  0.64 us (2%)
    pallas_call x1, Pallas kernels, on_device(): pl.pallas_call(functools.partial(kernel, n_chips, width, group, size ** (...  32.7 us
    pallas_call x1, Pallas kernels, on_device(): pl.pallas_call(hand_over, out_shape=tuple((jax.ShapeDtypeStruct(x.shape,...  1.07 us

profile of v2, /device:TPU:1, one launch (start us, length us, event | category | flops | bytes accessed | tf_op | source)
XLA Modules:
  0.0 34.4 jit_solution(16971739119970525020)
XLA Ops:
  0.6 32.7 %shard_map.94 = (bf16[128,4,8,128]{3,2,1,0:T(8,128)(2,1)S(1)}, bf16[128,4,128]{2,1,0:T(4,128)(2,1)S(1)}, bf16[128,4,128]{2,1,0:T(4,128)(2,1)S(1)}) custom-call(bf16[128,4,8,128]{3,2,1,0:T(8,128)(2,1)} %bitcast.6, bf16[128,4,128]{2,1,0:T(4,128)(2,1)} %k_hbm.1, bf16[128,4,128]{2,1,0:T(4,128)(2,1)} %v_hbm.1, bf16[128,4,8,128]{3,2,1,0:T(8,128)(2,1)} %bitcast.7, ...), custom_call_target="tpu_custom_call" | custom-call | tf_op jit(solution)/shard_map/pallas_call | solution.py:261
  33.4 1.1 %shard_map.95 = (bf16[128,4,8,128]{3,2,1,0:T(8,128)(2,1)}, bf16[128,4,128]{2,1,0:T(4,128)(2,1)}, bf16[128,4,128]{2,1,0:T(4,128)(2,1)}) custom-call(bf16[128,4,8,128]{3,2,1,0:T(8,128)(2,1)S(1)} %get-tuple-element.9.refs_0_, bf16[128,4,128]{2,1,0:T(4,128)(2,1)S(1)} %get-tuple-element.10.refs_1_, bf16[128,4,128]{2,1,0:T(4,128)(2,1)S(1)} %get-tuple-element.11.refs_2_), custom_call_target="tpu_custom_call" | custom-call | tf_op jit(solution)/shard_map/pallas_call | solution.py:301

commit v3 on v2

--- a/solution.py
+++ b/solution.py
@@ -24,8 +24,8 @@
            q_hbm, k_hbm, v_hbm, o_hbm, g_hbm, lse_hbm, doc_hbm,
            dq_out, dk_out, dv_out,
            qs, gs, os_, lse_in, docs, kin, vin, own_kv, kvb, bias, lse_b, dl_b, dq_acc, dq_send,
-           parts, d0, ret, rb0, rb1, rb2,
-           loc_sem, xs, xr, ks, kr0, kr1, fs, fr, rs0, rs1, rs2, rr0, rr1, rr2, dqs, dqr):
+           parts, near, far, ret0, ret1, ret2, rb0, rb1, rb2, pre, total,
+           loc_sem, xs, xr, ks, ks0, kr0, kr1, fs, fr, rs0, rs1, rs2, rr0, rr1, rr2, rp, dqs, dqr):
     me = lax.axis_index("seq")
     core = lax.rem(me, 2)
     chip = me // 2
@@ -38,14 +38,20 @@
     sibling = device(0, other)
 
     barrier = pltpu.get_barrier_semaphore()
-    pl.semaphore_signal(barrier, inc=1, device_id=sibling, device_id_type=MESH)
     pl.semaphore_signal(barrier, inc=1, device_id=device(-1, 0), device_id_type=MESH)
     pl.semaphore_signal(barrier, inc=1, device_id=device(-1, 1), device_id_type=MESH)
+    pl.semaphore_signal(barrier, inc=1, device_id=sibling, device_id_type=MESH)
 
     def remote(src, dst, send, recv, to):
         return pltpu.make_async_remote_copy(
             src_ref=src, dst_ref=dst, send_sem=send, recv_sem=recv, device_id=to, device_id_type=MESH
         )
+
+    def arrived(dst, sem):
+        remote(dst, dst, xs.at[0], sem, sibling).wait_recv()
+
+    def sent(src, sem):
+        remote(src, src, sem, xr.at[0], sibling).wait_send()
 
     local = [
         pltpu.make_async_copy(k_hbm, kin, loc_sem.at[0]),
@@ -62,31 +68,35 @@
         copy.start()
 
     local[0].wait()
+    own_kv[:, 0] = jnp.transpose(kin[...], (1, 0, 2))
     local[1].wait()
-    own_kv[:, 0] = jnp.transpose(kin[...], (1, 0, 2))
     own_kv[:, 1] = jnp.transpose(vin[...], (1, 0, 2))
-    for j in range(2):
-        kvb[0, j, core] = own_kv[2 * core + j]
 
     pl.semaphore_wait(barrier, 3)
 
-    sends = []
-    for j in range(2):
-        for x, which in enumerate((core, other)):
-            sends.append(
-                remote(own_kv.at[2 * which + j], kvb.at[1, j, core], ks.at[2 * j + x], kr1.at[j, core], device(1, which))
-            )
-    for copy in sends:
-        copy.start()
-    swaps = [
-        remote(lse_hbm.at[pl.ds(2 * other, 2)], lse_in.at[:, core], xs.at[6], xr.at[6], sibling),
-    ]
+    def half_of(n):
+        return (core, other)[n % 2]
+
+    def own(n):
+        j, which = n // 2, half_of(n)
+        return [
+            remote(own_kv.at[2 * which + j, p], kvb.at[1, j, core, p], ks.at[n, p], kr1.at[j, core, p], device(1, which))
+            for p in range(2)
+        ]
+
+    for n in range(3):
+        for copy in own(n):
+            copy.start()
+    swaps = [remote(lse_hbm.at[pl.ds(2 * other, 2)], lse_in.at[:, core], xs.at[6], xr.at[6], sibling)]
     for j in range(2):
         for i, (src, dst) in enumerate(((g_hbm, gs), (o_hbm, os_), (q_hbm, qs))):
             swaps.append(remote(src.at[:, 2 * other + j], dst.at[j, core], xs.at[3 * j + i], xr.at[3 * j + i], sibling))
-        swaps.append(remote(own_kv.at[2 * other + j], kvb.at[0, j, core], ks.at[4 + j], kr0.at[j], sibling))
+        swaps.append(remote(own_kv.at[2 * other + j], kvb.at[0, j, core], ks0.at[j], kr0.at[j], sibling))
     for copy in swaps:
         copy.start()
+
+    for j in range(2):
+        kvb[0, j, core] = own_kv[2 * core + j]
 
     local[2].wait()
 
@@ -118,16 +128,10 @@
         o = os_[j, half].reshape(rows, 128).astype(F32)
         dl_b[j, pl.ds(start, rows), :] = jnp.broadcast_to(jnp.sum(g * o, axis=-1, keepdims=True), (rows, 128))
 
-    def block(j, back, key_half, half, halves, first):
-        start = pl.multiple_of(half * rows, rows)
-        count = rows * halves
-        r = pl.ds(start, count)
-        if halves == 1:
-            q = qs[j, half].reshape(count, 128)
-            g = gs[j, half].reshape(count, 128)
-        else:
-            q = qs[j].reshape(count, 128)
-            g = gs[j].reshape(count, 128)
+    def block(j, back, key_half, half, first=False):
+        r = pl.ds(pl.multiple_of(half * rows, rows), rows)
+        q = qs[j, half].reshape(rows, 128)
+        g = gs[j, half].reshape(rows, 128)
         k = kvb[back, j, key_half, 0]
         v = kvb[back, j, key_half, 1]
         s = dot(q, k, NT)
@@ -147,97 +151,150 @@
 
     def own_step(j, carry):
         row_terms(j, core)
-        dk, dv = block(j, 0, core, core, 1, True)
+        dk, dv = block(j, 0, core, core, True)
         parts[0, j, 0] = dk
         parts[0, j, 1] = dv
         return carry
 
     lax.fori_loop(0, 2, own_step, 0)
 
-    def arrival(dst, sem):
-        return remote(dst, dst, fs.at[0], sem, sibling)
-
-    arrival(lse_in.at[:, other], xr.at[6]).wait_recv()
-
-    def sibling_step(j, carry):
-        for i, dst in enumerate((gs, os_, qs)):
-            arrival(dst.at[j, other], xr.at[3 * j + i]).wait_recv()
+    arrived(lse_in.at[:, other], xr.at[6])
+
+    def swap_terms(j):
+        for i, dst in enumerate((gs, os_)):
+            arrived(dst.at[j, other], xr.at[3 * j + i])
         row_terms(j, other)
-        arrival(kvb.at[0, j, other], kr0.at[j]).wait_recv()
-        dk, dv = block(j, 0, other, other, 1, True)
+
+    def sibling_keys(j, first):
+        arrived(qs.at[j, other], xr.at[3 * j + 2])
+        arrived(kvb.at[0, j, other], kr0.at[j])
+        dk, dv = block(j, 0, other, other, first)
         parts[1, j, 0] = dk
         parts[1, j, 1] = dv
-        dk, dv = block(j, 0, 0, 1, 1, False)
+
+    def late_rows(j):
+        dk, dv = block(j, 0, 0, 1)
         parts[core, j, 0] += dk
         parts[core, j, 1] += dv
-        ret[j] = parts[1, j].astype(BF16)
-        remote(ret.at[j], rb0.at[j], rs0.at[j], rr0.at[j], sibling).start()
-        return carry
-
-    lax.fori_loop(0, 2, sibling_step, 0)
-
-    def near_step(n, carry):
-        j = n // 2
-        a = jnp.where(lax.rem(n, 2) == 0, core, other)
-        arrival(kvb.at[1, j, a], kr1.at[j, a]).wait_recv()
-        remote(kvb.at[1, j, a], kvb.at[2, j, a], fs.at[n], fr.at[j, a], device(1, core)).start()
-        dk, dv = block(j, 1, a, 0, 2, False)
-        ret[2 + n, 0] = dk.astype(BF16)
-        ret[2 + n, 1] = dv.astype(BF16)
-        remote(ret.at[2 + n], rb1.at[2 * core + j], rs1.at[n], rr1.at[2 * core + j], device(-1, a)).start()
-        return carry
-
-    lax.fori_loop(0, 4, near_step, 0)
-
-    def far_step(n, carry):
-        j = n // 2
-        a = jnp.where(lax.rem(n, 2) == 0, core, other)
-        arrival(kvb.at[2, j, a], fr.at[j, a]).wait_recv()
-        dk, dv = block(j, 2, a, 0, 1, False)
-        ret[6 + n, 0] = dk.astype(BF16)
-        ret[6 + n, 1] = dv.astype(BF16)
+        ret0[j] = parts[1, j].astype(BF16)
+        remote(ret0.at[j], rb0.at[j], rs0.at[j], rr0.at[j], sibling).start()
+
+    def forward(n, p):
+        j, a = n // 2, half_of(n)
+        arrived(kvb.at[1, j, a, p], kr1.at[j, a, p])
+        remote(kvb.at[1, j, a, p], kvb.at[2, j, a, p], fs.at[n, p], fr.at[j, a, p], device(1, core)).start()
+
+    def give_near(n, p):
+        j, a = n // 2, half_of(n)
+        remote(ret1.at[n, p], rb1.at[2 * core + j, p], rs1.at[n, p], rr1.at[2 * core + j, p], device(-1, a)).start()
+
+    def near_own(n):
+        dk, dv = block(n // 2, 1, half_of(n), core)
+        near[n, 0] = dk
+        near[n, 1] = dv
+
+    def near_other(n, first=False):
+        dk, dv = block(n // 2, 1, half_of(n), other, first)
+        near[n, 0] += dk
+        near[n, 1] += dv
+
+    def far_block(n):
+        j, a = n // 2, half_of(n)
+        for p in range(2):
+            arrived(kvb.at[2, j, a, p], fr.at[j, a, p])
+        dk, dv = block(j, 2, a, 0)
+        far[0] = dk
+        far[1] = dv
 
         @pl.when(a == 1)
         def _():
-            dk2, dv2 = block(j, 2, a, 1, 1, False)
-            ret[6 + n, 0] = (dk + dk2).astype(BF16)
-            ret[6 + n, 1] = (dv + dv2).astype(BF16)
-
-        remote(ret.at[6 + n], rb2.at[2 * core + j], rs2.at[n], rr2.at[2 * core + j], device(-2, a)).start()
-
-        @pl.when(lax.rem(n, 2) == 1)
-        def _():
-            mine = dq_acc[j, pl.ds(pl.multiple_of(core * rows, rows), rows), :] * scale
-            theirs = dq_acc[j, pl.ds(pl.multiple_of(other * rows, rows), rows), :] * scale
-            dq_send[j] = theirs.astype(BF16).reshape(width, group, 128)
-            remote(dq_send.at[j], dq_out.at[:, 2 * core + j], dqs.at[j], dqr.at[j], sibling).start()
-            dq_out[:, 2 * core + j] = mine.astype(BF16).reshape(width, group, 128)
-
-        return carry
-
-    lax.fori_loop(0, 4, far_step, 0)
+            dk2, dv2 = block(j, 2, a, 1)
+            far[0] += dk2
+            far[1] += dv2
+
+        for p in range(2):
+            ret2[n, p] = far[p].astype(BF16)
+            if n == 0:
+                remote(ret2.at[0, p], rb2.at[p], rs2.at[0, p], rr2.at[p], device(-2, a)).start()
+            else:
+                remote(ret2.at[n, p], pre.at[n, p], rs2.at[n, p], rp.at[n, p], device(-1, core)).start()
+
+    def pass_on(n, p):
+        arrived(pre.at[n, p], rp.at[n, p])
+        ret1[n, p] = (near[n, p] + pre[n, p].astype(F32)).astype(BF16)
+        give_near(n, p)
+
+    def give_queries(j):
+        theirs = dq_acc[j, pl.ds(pl.multiple_of(other * rows, rows), rows), :] * scale
+        dq_send[j] = theirs.astype(BF16).reshape(width, group, 128)
+        remote(dq_send.at[j], dq_out.at[:, 2 * core + j], dqs.at[j], dqr.at[j], sibling).start()
+        mine = dq_acc[j, pl.ds(pl.multiple_of(core * rows, rows), rows), :] * scale
+        dq_out[:, 2 * core + j] = mine.astype(BF16).reshape(width, group, 128)
+
+    swap_terms(0)
+    sibling_keys(0, True)
+    forward(0, 0)
+    late_rows(0)
+    forward(0, 1)
+    for copy in own(3):
+        copy.start()
+    near_own(0)
+    forward(1, 0)
+    near_other(0)
+    for p in range(2):
+        ret1[0, p] = near[0, p].astype(BF16)
+        give_near(0, p)
+    forward(1, 1)
+    near_own(1)
+    near_other(1)
+    forward(2, 0)
+    swap_terms(1)
+    forward(2, 1)
+    sibling_keys(1, True)
+    near_own(2)
+    near_other(2)
+    far_block(0)
+    forward(3, 0)
+    late_rows(1)
+    forward(3, 1)
+    near_own(3)
+    near_other(3)
+    far_block(1)
+    give_queries(0)
+    far_block(2)
+    far_block(3)
+    give_queries(1)
+    for n in range(1, 4):
+        for p in range(2):
+            pass_on(n, p)
+
+    for n in range(4):
+        j = n // 2
+        h = 2 * half_of(n) + j
+        if n % 2 == 1:
+            arrived(rb0.at[j], rr0.at[j])
+        for p in range(2):
+            arrived(rb1.at[h, p], rr1.at[h, p])
+            acc = rb1[h, p].astype(F32) + (parts[0, j, p] if n % 2 == 0 else rb0[j, p].astype(F32))
+            if n == 0:
+                arrived(rb2.at[p], rr2.at[p])
+                acc = acc + rb2[p].astype(F32)
+            total[p, h] = acc.T
+    dk_out[...] = jnp.transpose(total[0], (1, 0, 2)).astype(BF16)
+    dv_out[...] = jnp.transpose(total[1], (1, 0, 2)).astype(BF16)
 
     for j in range(2):
-        arrival(rb0.at[j], rr0.at[j]).wait_recv()
-        d0[2 * core + j] = parts[0, j]
-        d0[2 * other + j] = rb0[j].astype(F32)
-    for h in range(4):
-        arrival(rb1.at[h], rr1.at[h]).wait_recv()
-    for h in range(4):
-        arrival(rb2.at[h], rr2.at[h]).wait_recv()
-    for i, out in enumerate((dk_out, dv_out)):
-        heads = [(d0[h, i] + rb1[h, i].astype(F32) + rb2[h, i].astype(F32)).T for h in range(4)]
-        out[...] = jnp.transpose(jnp.stack(heads), (1, 0, 2)).astype(BF16)
-
-    for j in range(2):
-        remote(dq_send.at[j], dq_out.at[:, 2 * other + j], dqs.at[j], dqr.at[j], sibling).wait()
-        remote(ret.at[j], rb0.at[j], rs0.at[j], rr0.at[j], sibling).wait_send()
-    for copy in sends + swaps:
+        arrived(dq_out.at[:, 2 * other + j], dqr.at[j])
+        sent(dq_send.at[j], dqs.at[j])
+        sent(ret0.at[j], rs0.at[j])
+    for copy in swaps:
         copy.wait_send()
     for n in range(4):
-        remote(kvb.at[1, 0, 0], kvb.at[2, 0, 0], fs.at[n], fr.at[0, 0], sibling).wait_send()
-        remote(ret.at[2 + n], rb1.at[0], rs1.at[n], rr1.at[0], sibling).wait_send()
-        remote(ret.at[6 + n], rb2.at[0], rs2.at[n], rr2.at[0], sibling).wait_send()
+        for p in range(2):
+            sent(own_kv.at[0, p], ks.at[n, p])
+            sent(kvb.at[1, 0, 0, p], fs.at[n, p])
+            sent(ret1.at[n, p], rs1.at[n, p])
+            sent(ret2.at[n, p], rs2.at[n, p])
 
 
 def hand_over(*refs):
@@ -283,13 +340,19 @@
             pltpu.VMEM((2, 2 * rows, size), F32),
             pltpu.VMEM((2, width, group, size), BF16),
             pltpu.VMEM((2, 2, 2, size, width), F32),
-            pltpu.VMEM((kv, 2, size, width), F32),
-            pltpu.VMEM((10, 2, size, width), BF16),
+            pltpu.VMEM((4, 2, size, width), F32),
+            pltpu.VMEM((2, size, width), F32),
+            pltpu.VMEM((2, 2, size, width), BF16),
+            pltpu.VMEM((4, 2, size, width), BF16),
+            pltpu.VMEM((4, 2, size, width), BF16),
             pltpu.VMEM((2, 2, size, width), BF16),
             pltpu.VMEM((kv, 2, size, width), BF16),
-            pltpu.VMEM((kv, 2, size, width), BF16),
-            dma((10,)), dma((7,)), dma((7,)), dma((6,)), dma((2,)), dma((2, 2)), dma((4,)), dma((2, 2)),
-            dma((2,)), dma((4,)), dma((4,)), dma((2,)), dma((4,)), dma((4,)), dma((2,)), dma((2,)),
+            pltpu.VMEM((2, size, width), BF16),
+            pltpu.VMEM((4, 2, size, width), BF16),
+            pltpu.VMEM((2, kv, width, size), F32),
+            dma((10,)), dma((7,)), dma((7,)), dma((4, 2)), dma((2,)), dma((2,)), dma((2, 2, 2)), dma((4, 2)),
+            dma((2, 2, 2)), dma((2,)), dma((4, 2)), dma((4, 2)), dma((2,)), dma((kv, 2)), dma((2,)), dma((4, 2)),
+            dma((2,)), dma((2,)),
         ],
         compiler_params=pltpu.CompilerParams(
             collective_id=0, has_side_effects=True, vmem_limit_bytes=56 * 2**20

time: 34.9 us -> 33.5 us (0.960)
  Pallas kernels: 33.8 us -> 32.7 us
    pallas_call x1, Pallas kernels: 32.7 us -> 31.7 us  [on_device(): pl.pallas_call(functools.partial(kernel, n_chips, width, group, size ** (...]
where the time goes in v3:
time: 33.5 us; the launch traced here: 33.4 us
  Pallas kernels  32.7 us (98%)
  between operations  0.64 us (2%)
    pallas_call x1, Pallas kernels, on_device(): pl.pallas_call(functools.partial(kernel, n_chips, width, group, size ** (...  31.7 us
    pallas_call x1, Pallas kernels, on_device(): pl.pallas_call(hand_over, out_shape=tuple((jax.ShapeDtypeStruct(x.shape,...  1.07 us

profile of v3, /device:TPU:1, one launch (start us, length us, event | category | flops | bytes accessed | tf_op | source)
XLA Modules:
  0.0 33.4 jit_solution(16022687749404478826)
XLA Ops:
  0.6 31.7 %shard_map.94 = (bf16[128,4,8,128]{3,2,1,0:T(8,128)(2,1)S(1)}, bf16[128,4,128]{2,1,0:T(4,128)(2,1)S(1)}, bf16[128,4,128]{2,1,0:T(4,128)(2,1)S(1)}) custom-call(bf16[128,4,8,128]{3,2,1,0:T(8,128)(2,1)} %bitcast.6, bf16[128,4,128]{2,1,0:T(4,128)(2,1)} %k_hbm.1, bf16[128,4,128]{2,1,0:T(4,128)(2,1)} %v_hbm.1, bf16[128,4,8,128]{3,2,1,0:T(8,128)(2,1)} %bitcast.7, ...), custom_call_target="tpu_custom_call" | custom-call | tf_op jit(solution)/shard_map/pallas_call | solution.py:318
  32.3 1.1 %shard_map.95 = (bf16[128,4,8,128]{3,2,1,0:T(8,128)(2,1)}, bf16[128,4,128]{2,1,0:T(4,128)(2,1)}, bf16[128,4,128]{2,1,0:T(4,128)(2,1)}) custom-call(bf16[128,4,8,128]{3,2,1,0:T(8,128)(2,1)S(1)} %get-tuple-element.9.refs_0_, bf16[128,4,128]{2,1,0:T(4,128)(2,1)S(1)} %get-tuple-element.10.refs_1_, bf16[128,4,128]{2,1,0:T(4,128)(2,1)S(1)} %get-tuple-element.11.refs_2_), custom_call_target="tpu_custom_call" | custom-call | tf_op jit(solution)/shard_map/pallas_call | solution.py:364

commit v4 on v3

--- a/solution.py
+++ b/solution.py
@@ -23,9 +23,11 @@
 def kernel(n_chips, width, group, scale,
            q_hbm, k_hbm, v_hbm, o_hbm, g_hbm, lse_hbm, doc_hbm,
            dq_out, dk_out, dv_out,
-           qs, gs, os_, lse_in, docs, kin, vin, own_kv, kvb, bias, lse_b, dl_b, dq_acc, dq_send,
+           qs, gs, os_, lse_in, docs, kin, vin, own_kv, kvb, bias0, bias1, bias2, lse_b0, lse_b1, dl_b0, dl_b1, dq_acc0, dq_acc1, dq_send,
            parts, near, far, ret0, ret1, ret2, rb0, rb1, rb2, pre, total,
            loc_sem, xs, xr, ks, ks0, kr0, kr1, fs, fr, rs0, rs1, rs2, rr0, rr1, rr2, rp, dqs, dqr):
+    lse_b, dl_b, dq_acc = (lse_b0, lse_b1), (dl_b0, dl_b1), (dq_acc0, dq_acc1)
+    bias = (bias0, bias1, bias2)
     me = lax.axis_index("seq")
     core = lax.rem(me, 2)
     chip = me // 2
@@ -36,10 +38,16 @@
         return {"seq": lax.rem(chip + step + n_chips, n_chips) * 2 + which}
 
     sibling = device(0, other)
+    has_prev, has_next = chip > 0, chip < n_chips - 1
+    has_prev2, has_next2 = chip > 1, chip < n_chips - 2
 
     barrier = pltpu.get_barrier_semaphore()
-    pl.semaphore_signal(barrier, inc=1, device_id=device(-1, 0), device_id_type=MESH)
-    pl.semaphore_signal(barrier, inc=1, device_id=device(-1, 1), device_id_type=MESH)
+
+    @pl.when(has_prev)
+    def _():
+        pl.semaphore_signal(barrier, inc=1, device_id=device(-1, 0), device_id_type=MESH)
+        pl.semaphore_signal(barrier, inc=1, device_id=device(-1, 1), device_id_type=MESH)
+
     pl.semaphore_signal(barrier, inc=1, device_id=sibling, device_id_type=MESH)
 
     def remote(src, dst, send, recv, to):
@@ -47,11 +55,43 @@
             src_ref=src, dst_ref=dst, send_sem=send, recv_sem=recv, device_id=to, device_id_type=MESH
         )
 
-    def arrived(dst, sem):
-        remote(dst, dst, xs.at[0], sem, sibling).wait_recv()
-
-    def sent(src, sem):
-        remote(src, src, sem, xr.at[0], sibling).wait_send()
+    def arrived(dst, sem, there=None):
+        def wait():
+            remote(dst, dst, xs.at[0], sem, sibling).wait_recv()
+
+        wait() if there is None else pl.when(there)(wait)
+
+    def sent(src, sem, there=None):
+        def wait():
+            remote(src, src, sem, xr.at[0], sibling).wait_send()
+
+        wait() if there is None else pl.when(there)(wait)
+
+    def start(copies, there):
+        @pl.when(there)
+        def _():
+            for copy in copies:
+                copy.start()
+
+    @pl.when(chip == 0)
+    def _():
+        kvb[1] = jnp.zeros_like(kvb[1])
+
+    @pl.when(jnp.logical_not(has_prev2))
+    def _():
+        kvb[2] = jnp.zeros_like(kvb[2])
+
+    @pl.when(jnp.logical_not(has_next))
+    def _():
+        rb1[...] = jnp.zeros_like(rb1)
+
+    @pl.when(jnp.logical_not(has_next & has_prev))
+    def _():
+        pre[...] = jnp.zeros_like(pre)
+
+    @pl.when(jnp.logical_not(has_next2))
+    def _():
+        rb2[...] = jnp.zeros_like(rb2)
 
     local = [
         pltpu.make_async_copy(k_hbm, kin, loc_sem.at[0]),
@@ -72,7 +112,7 @@
     local[1].wait()
     own_kv[:, 1] = jnp.transpose(vin[...], (1, 0, 2))
 
-    pl.semaphore_wait(barrier, 3)
+    pl.semaphore_wait(barrier, jnp.where(has_next, 3, 1))
 
     def half_of(n):
         return (core, other)[n % 2]
@@ -84,9 +124,7 @@
             for p in range(2)
         ]
 
-    for n in range(3):
-        for copy in own(n):
-            copy.start()
+    start(own(0) + own(1) + own(2), has_next)
     swaps = [remote(lse_hbm.at[pl.ds(2 * other, 2)], lse_in.at[:, core], xs.at[6], xr.at[6], sibling)]
     for j in range(2):
         for i, (src, dst) in enumerate(((g_hbm, gs), (o_hbm, os_), (q_hbm, qs))):
@@ -100,10 +138,7 @@
 
     local[2].wait()
 
-    def mask_step(index, carry):
-        back = index // 4
-        key_half = lax.rem(index // 2, 2)
-        query_half = lax.rem(index, 2)
+    def mask(back, query_half, key_half):
         key_chip = chip - back
         key_row = lax.rem(key_chip + n_chips, n_chips) * 2 + key_half
         query_row = chip * 2 + query_half
@@ -113,20 +148,20 @@
         t = lax.broadcasted_iota(jnp.int32, (width, width), 0) + query_row * width
         p = lax.broadcasted_iota(jnp.int32, (width, width), 1) + (key_chip * 2 + key_half) * width
         live = (query_col == key_doc) & (p <= t) & (p >= 0)
-        block = jnp.where(live, 0.0, -jnp.inf).astype(F32)
-        wide = jnp.broadcast_to(block[:, None, :], (width, group, width)).reshape(rows, width)
-        bias[back, key_half, pl.ds(pl.multiple_of(query_half * rows, rows), rows), :] = wide
-        return carry
-
-    lax.fori_loop(0, 12, mask_step, 0)
+        value = jnp.where(live, 0.0, -jnp.inf).astype(F32)
+        wide = jnp.broadcast_to(value[:, None, :], (width, group, width)).reshape(rows, width)
+        bias[back][key_half, query_half * rows:(query_half + 1) * rows, :] = wide
+
+    for query_half, key_half in ((0, 0), (1, 0), (1, 1)):
+        mask(0, query_half, key_half)
 
     def row_terms(j, half):
         start = pl.multiple_of(half * rows, rows)
         row = lse_in[j, half] * LOG2E
-        lse_b[j, pl.ds(start, rows), :] = jnp.broadcast_to(row.T[:, :, None], (width, group, 128)).reshape(rows, 128)
+        lse_b[j][pl.ds(start, rows), :] = jnp.broadcast_to(row.T[:, :, None], (width, group, 128)).reshape(rows, 128)
         g = gs[j, half].reshape(rows, 128).astype(F32)
         o = os_[j, half].reshape(rows, 128).astype(F32)
-        dl_b[j, pl.ds(start, rows), :] = jnp.broadcast_to(jnp.sum(g * o, axis=-1, keepdims=True), (rows, 128))
+        dl_b[j][pl.ds(start, rows), :] = jnp.broadcast_to(jnp.sum(g * o, axis=-1, keepdims=True), (rows, 128))
 
     def block(j, back, key_half, half, first=False):
         r = pl.ds(pl.multiple_of(half * rows, rows), rows)
@@ -136,34 +171,33 @@
         v = kvb[back, j, key_half, 1]
         s = dot(q, k, NT)
         dp = dot(g, v, NT)
-        p = jnp.exp2(s * (scale * LOG2E) - lse_b[j, r, :] + bias[back, key_half, r, :])
-        ds = (p * (dp - dl_b[j, r, :])).astype(BF16)
+        p = jnp.exp2(s * (scale * LOG2E) - lse_b[j][r, :] + bias[back][key_half, r, :])
+        ds = (p * (dp - dl_b[j][r, :])).astype(BF16)
         p = p.astype(BF16)
         term = dot(ds, k, NN)
         if first:
-            dq_acc[j, r, :] = term
+            dq_acc[j][r, :] = term
         else:
-            dq_acc[j, r, :] += term
+            dq_acc[j][r, :] += term
         return dot(q, ds, TN) * scale, dot(g, p, TN)
 
     for copy in local[3:]:
         copy.wait()
 
-    def own_step(j, carry):
+    for j in range(2):
         row_terms(j, core)
+    for j in range(2):
+        mask(1, j, 0)
+        mask(1, j, 1)
         dk, dv = block(j, 0, core, core, True)
         parts[0, j, 0] = dk
         parts[0, j, 1] = dv
-        return carry
-
-    lax.fori_loop(0, 2, own_step, 0)
 
     arrived(lse_in.at[:, other], xr.at[6])
 
-    def swap_terms(j):
+    def swap_wait(j):
         for i, dst in enumerate((gs, os_)):
             arrived(dst.at[j, other], xr.at[3 * j + i])
-        row_terms(j, other)
 
     def sibling_keys(j, first):
         arrived(qs.at[j, other], xr.at[3 * j + 2])
@@ -181,12 +215,14 @@
 
     def forward(n, p):
         j, a = n // 2, half_of(n)
-        arrived(kvb.at[1, j, a, p], kr1.at[j, a, p])
-        remote(kvb.at[1, j, a, p], kvb.at[2, j, a, p], fs.at[n, p], fr.at[j, a, p], device(1, core)).start()
+        arrived(kvb.at[1, j, a, p], kr1.at[j, a, p], has_prev)
+        copy = remote(kvb.at[1, j, a, p], kvb.at[2, j, a, p], fs.at[n, p], fr.at[j, a, p], device(1, core))
+        start([copy], has_prev & has_next)
 
     def give_near(n, p):
         j, a = n // 2, half_of(n)
-        remote(ret1.at[n, p], rb1.at[2 * core + j, p], rs1.at[n, p], rr1.at[2 * core + j, p], device(-1, a)).start()
+        copy = remote(ret1.at[n, p], rb1.at[2 * core + j, p], rs1.at[n, p], rr1.at[2 * core + j, p], device(-1, a))
+        start([copy], has_prev)
 
     def near_own(n):
         dk, dv = block(n // 2, 1, half_of(n), core)
@@ -201,7 +237,7 @@
     def far_block(n):
         j, a = n // 2, half_of(n)
         for p in range(2):
-            arrived(kvb.at[2, j, a, p], fr.at[j, a, p])
+            arrived(kvb.at[2, j, a, p], fr.at[j, a, p], has_prev2)
         dk, dv = block(j, 2, a, 0)
         far[0] = dk
         far[1] = dv
@@ -215,29 +251,32 @@
         for p in range(2):
             ret2[n, p] = far[p].astype(BF16)
             if n == 0:
-                remote(ret2.at[0, p], rb2.at[p], rs2.at[0, p], rr2.at[p], device(-2, a)).start()
+                copy = remote(ret2.at[0, p], rb2.at[p], rs2.at[0, p], rr2.at[p], device(-2, a))
             else:
-                remote(ret2.at[n, p], pre.at[n, p], rs2.at[n, p], rp.at[n, p], device(-1, core)).start()
+                copy = remote(ret2.at[n, p], pre.at[n, p], rs2.at[n, p], rp.at[n, p], device(-1, core))
+            start([copy], has_prev2)
 
     def pass_on(n, p):
-        arrived(pre.at[n, p], rp.at[n, p])
+        arrived(pre.at[n, p], rp.at[n, p], has_prev & has_next)
         ret1[n, p] = (near[n, p] + pre[n, p].astype(F32)).astype(BF16)
         give_near(n, p)
 
     def give_queries(j):
-        theirs = dq_acc[j, pl.ds(pl.multiple_of(other * rows, rows), rows), :] * scale
+        theirs = dq_acc[j][pl.ds(pl.multiple_of(other * rows, rows), rows), :] * scale
         dq_send[j] = theirs.astype(BF16).reshape(width, group, 128)
         remote(dq_send.at[j], dq_out.at[:, 2 * core + j], dqs.at[j], dqr.at[j], sibling).start()
-        mine = dq_acc[j, pl.ds(pl.multiple_of(core * rows, rows), rows), :] * scale
+        mine = dq_acc[j][pl.ds(pl.multiple_of(core * rows, rows), rows), :] * scale
         dq_out[:, 2 * core + j] = mine.astype(BF16).reshape(width, group, 128)
 
-    swap_terms(0)
+    swap_wait(0)
+    row_terms(0, other)
     sibling_keys(0, True)
     forward(0, 0)
     late_rows(0)
+    for query_half, key_half in ((0, 0), (0, 1), (1, 1)):
+        mask(2, query_half, key_half)
     forward(0, 1)
-    for copy in own(3):
-        copy.start()
+    start(own(3), has_next)
     near_own(0)
     forward(1, 0)
     near_other(0)
@@ -245,10 +284,11 @@
         ret1[0, p] = near[0, p].astype(BF16)
         give_near(0, p)
     forward(1, 1)
+    swap_wait(1)
     near_own(1)
+    row_terms(1, other)
     near_other(1)
     forward(2, 0)
-    swap_terms(1)
     forward(2, 1)
     sibling_keys(1, True)
     near_own(2)
@@ -274,10 +314,10 @@
         if n % 2 == 1:
             arrived(rb0.at[j], rr0.at[j])
         for p in range(2):
-            arrived(rb1.at[h, p], rr1.at[h, p])
+            arrived(rb1.at[h, p], rr1.at[h, p], has_next)
             acc = rb1[h, p].astype(F32) + (parts[0, j, p] if n % 2 == 0 else rb0[j, p].astype(F32))
             if n == 0:
-                arrived(rb2.at[p], rr2.at[p])
+                arrived(rb2.at[p], rr2.at[p], has_next2)
                 acc = acc + rb2[p].astype(F32)
             total[p, h] = acc.T
     dk_out[...] = jnp.transpose(total[0], (1, 0, 2)).astype(BF16)
@@ -291,10 +331,10 @@
         copy.wait_send()
     for n in range(4):
         for p in range(2):
-            sent(own_kv.at[0, p], ks.at[n, p])
-            sent(kvb.at[1, 0, 0, p], fs.at[n, p])
-            sent(ret1.at[n, p], rs1.at[n, p])
-            sent(ret2.at[n, p], rs2.at[n, p])
+            sent(own_kv.at[0, p], ks.at[n, p], has_next)
+            sent(kvb.at[1, 0, 0, p], fs.at[n, p], has_prev & has_next)
+            sent(ret1.at[n, p], rs1.at[n, p], has_prev)
+            sent(ret2.at[n, p], rs2.at[n, p], has_prev2)
 
 
 def hand_over(*refs):
@@ -334,10 +374,8 @@
             pltpu.VMEM(keys.shape, BF16),
             pltpu.VMEM((kv, 2, width, size), BF16),
             pltpu.VMEM((3, 2, 2, 2, width, size), BF16),
-            pltpu.VMEM((3, 2, 2 * rows, width), F32),
-            pltpu.VMEM((2, 2 * rows, 128), F32),
-            pltpu.VMEM((2, 2 * rows, 128), F32),
-            pltpu.VMEM((2, 2 * rows, size), F32),
+            *[pltpu.VMEM((2, 2 * rows, width), F32)] * 3,
+            *[pltpu.VMEM((2 * rows, 128), F32)] * 6,
             pltpu.VMEM((2, width, group, size), BF16),
             pltpu.VMEM((2, 2, 2, size, width), F32),
             pltpu.VMEM((4, 2, size, width), F32),

time: 33.5 us -> 30.1 us (0.90)
  the two profiles are of different devices: /device:TPU:1 before, /device:TPU:77 now
where the time goes in v4:
time: 30.1 us; the launch traced here: 30 us
  Pallas kernels  29.4 us (98%)
  between operations  0.64 us (2%)
    pallas_call x1, Pallas kernels, on_device(): pl.pallas_call(functools.partial(kernel, n_chips, width, group, size ** (...  28.3 us
    pallas_call x1, Pallas kernels, on_device(): pl.pallas_call(hand_over, out_shape=tuple((jax.ShapeDtypeStruct(x.shape,...  1.07 us

profile of v4, /device:TPU:77, one launch (start us, length us, event | category | flops | bytes accessed | tf_op | source)
XLA Modules:
  0.0 30.0 jit_solution(7595503521590033880)
XLA Ops:
  0.6 28.3 %shard_map.94 = (bf16[128,4,8,128]{3,2,1,0:T(8,128)(2,1)S(1)}, bf16[128,4,128]{2,1,0:T(4,128)(2,1)S(1)}, bf16[128,4,128]{2,1,0:T(4,128)(2,1)S(1)}) custom-call(bf16[128,4,8,128]{3,2,1,0:T(8,128)(2,1)} %bitcast.6, bf16[128,4,128]{2,1,0:T(4,128)(2,1)} %k_hbm.1, bf16[128,4,128]{2,1,0:T(4,128)(2,1)} %v_hbm.1, bf16[128,4,8,128]{3,2,1,0:T(8,128)(2,1)} %bitcast.7, ...), custom_call_target="tpu_custom_call" | custom-call | tf_op jit(solution)/shard_map/pallas_call | solution.py:358
  28.9 1.1 %shard_map.95 = (bf16[128,4,8,128]{3,2,1,0:T(8,128)(2,1)}, bf16[128,4,128]{2,1,0:T(4,128)(2,1)}, bf16[128,4,128]{2,1,0:T(4,128)(2,1)}) custom-call(bf16[128,4,8,128]{3,2,1,0:T(8,128)(2,1)S(1)} %get-tuple-element.9.refs_0_, bf16[128,4,128]{2,1,0:T(4,128)(2,1)S(1)} %get-tuple-element.10.refs_1_, bf16[128,4,128]{2,1,0:T(4,128)(2,1)S(1)} %get-tuple-element.11.refs_2_), custom_call_target="tpu_custom_call" | custom-call | tf_op jit(solution)/shard_map/pallas_call | solution.py:402

commit v5 on v4

--- a/solution.py
+++ b/solution.py
@@ -13,6 +13,7 @@
 NT = (((1,), (1,)), ((), ()))
 NN = (((1,), (0,)), ((), ()))
 TN = (((0,), (0,)), ((), ()))
+DIRECT = (0,)
 LOG2E = 1.4426950408889634
 
 
@@ -24,7 +25,7 @@
            q_hbm, k_hbm, v_hbm, o_hbm, g_hbm, lse_hbm, doc_hbm,
            dq_out, dk_out, dv_out,
            qs, gs, os_, lse_in, docs, kin, vin, own_kv, kvb, bias0, bias1, bias2, lse_b0, lse_b1, dl_b0, dl_b1, dq_acc0, dq_acc1, dq_send,
-           parts, near, far, ret0, ret1, ret2, rb0, rb1, rb2, pre, total,
+           parts, near, probs, ret0, ret1, ret2, rb0, rb1, rb2, pre, total,
            loc_sem, xs, xr, ks, ks0, kr0, kr1, fs, fr, rs0, rs1, rs2, rr0, rr1, rr2, rp, dqs, dqr):
     lse_b, dl_b, dq_acc = (lse_b0, lse_b1), (dl_b0, dl_b1), (dq_acc0, dq_acc1)
     bias = (bias0, bias1, bias2)
@@ -234,24 +235,42 @@
         near[n, 0] += dk
         near[n, 1] += dv
 
+    def near_done(n):
+        if n in DIRECT:
+            for p in range(2):
+                ret1[n, p] = near[n, p].astype(BF16)
+                give_near(n, p)
+
+    def far_probs(j, key_half, half):
+        r = pl.ds(half * rows, rows)
+        g = gs[j, half].reshape(rows, 128)
+        s = dot(qs[j, half].reshape(rows, 128), kvb[2, j, key_half, 0], NT)
+        p = jnp.exp2(s * (scale * LOG2E) - lse_b[j][r, :] + bias[2][key_half, r, :])
+        probs[r, :] = p
+        return dot(g, p.astype(BF16), TN)
+
+    def far_scores(j, key_half, half):
+        r = pl.ds(half * rows, rows)
+        dp = dot(gs[j, half].reshape(rows, 128), kvb[2, j, key_half, 1], NT)
+        ds = (probs[r, :] * (dp - dl_b[j][r, :])).astype(BF16)
+        dq_acc[j][r, :] += dot(ds, kvb[2, j, key_half, 0], NN)
+        return dot(qs[j, half].reshape(rows, 128), ds, TN) * scale
+
     def far_block(n):
         j, a = n // 2, half_of(n)
-        for p in range(2):
-            arrived(kvb.at[2, j, a, p], fr.at[j, a, p], has_prev2)
-        dk, dv = block(j, 2, a, 0)
-        far[0] = dk
-        far[1] = dv
-
-        @pl.when(a == 1)
-        def _():
-            dk2, dv2 = block(j, 2, a, 1)
-            far[0] += dk2
-            far[1] += dv2
-
-        for p in range(2):
-            ret2[n, p] = far[p].astype(BF16)
-            if n == 0:
-                copy = remote(ret2.at[0, p], rb2.at[p], rs2.at[0, p], rr2.at[p], device(-2, a))
+        for p, part in ((1, far_probs), (0, far_scores)):
+            arrived(kvb.at[2, j, a, 1 - p], fr.at[j, a, 1 - p], has_prev2)
+
+            @pl.when(a == 0)
+            def _():
+                ret2[n, p] = part(j, a, 0).astype(BF16)
+
+            @pl.when(a == 1)
+            def _():
+                ret2[n, p] = (part(j, a, 0) + part(j, a, 1)).astype(BF16)
+
+            if n in DIRECT:
+                copy = remote(ret2.at[n, p], rb2.at[n, p], rs2.at[n, p], rr2.at[n, p], device(-2, a))
             else:
                 copy = remote(ret2.at[n, p], pre.at[n, p], rs2.at[n, p], rp.at[n, p], device(-1, core))
             start([copy], has_prev2)
@@ -280,61 +299,68 @@
     near_own(0)
     forward(1, 0)
     near_other(0)
-    for p in range(2):
-        ret1[0, p] = near[0, p].astype(BF16)
-        give_near(0, p)
+    near_done(0)
     forward(1, 1)
     swap_wait(1)
     near_own(1)
     row_terms(1, other)
     near_other(1)
+    near_done(1)
     forward(2, 0)
     forward(2, 1)
     sibling_keys(1, True)
     near_own(2)
     near_other(2)
+    near_done(2)
     far_block(0)
     forward(3, 0)
     late_rows(1)
     forward(3, 1)
     near_own(3)
     near_other(3)
+    near_done(3)
     far_block(1)
     give_queries(0)
     far_block(2)
     far_block(3)
     give_queries(1)
-    for n in range(1, 4):
-        for p in range(2):
-            pass_on(n, p)
-
     for n in range(4):
-        j = n // 2
-        h = 2 * half_of(n) + j
-        if n % 2 == 1:
-            arrived(rb0.at[j], rr0.at[j])
-        for p in range(2):
-            arrived(rb1.at[h, p], rr1.at[h, p], has_next)
-            acc = rb1[h, p].astype(F32) + (parts[0, j, p] if n % 2 == 0 else rb0[j, p].astype(F32))
-            if n == 0:
-                arrived(rb2.at[p], rr2.at[p], has_next2)
-                acc = acc + rb2[p].astype(F32)
-            total[p, h] = acc.T
-    dk_out[...] = jnp.transpose(total[0], (1, 0, 2)).astype(BF16)
-    dv_out[...] = jnp.transpose(total[1], (1, 0, 2)).astype(BF16)
-
-    for j in range(2):
+        for p in (1, 0):
+            if n not in DIRECT:
+                pass_on(n, p)
+
+    for j in range(2):
+        arrived(rb0.at[j], rr0.at[j])
         arrived(dq_out.at[:, 2 * other + j], dqr.at[j])
         sent(dq_send.at[j], dqs.at[j])
         sent(ret0.at[j], rs0.at[j])
     for copy in swaps:
         copy.wait_send()
+
+    def finish(n, p):
+        j = n // 2
+        h = 2 * half_of(n) + j
+        if True:
+            arrived(rb1.at[h, p], rr1.at[h, p], has_next)
+            acc = rb1[h, p].astype(F32) + (parts[0, j, p] if n % 2 == 0 else rb0[j, p].astype(F32))
+            if n in DIRECT:
+                arrived(rb2.at[n, p], rr2.at[n, p], has_next2)
+                acc = acc + rb2[n, p].astype(F32)
+            total[p, h] = acc.T
+
+    for n in range(3):
+        for p in (1, 0):
+            finish(n, p)
+    finish(3, 1)
+    dv_out[...] = jnp.transpose(total[1], (1, 0, 2)).astype(BF16)
     for n in range(4):
         for p in range(2):
             sent(own_kv.at[0, p], ks.at[n, p], has_next)
             sent(kvb.at[1, 0, 0, p], fs.at[n, p], has_prev & has_next)
             sent(ret1.at[n, p], rs1.at[n, p], has_prev)
             sent(ret2.at[n, p], rs2.at[n, p], has_prev2)
+    finish(3, 0)
+    dk_out[...] = jnp.transpose(total[0], (1, 0, 2)).astype(BF16)
 
 
 def hand_over(*refs):
@@ -379,17 +405,17 @@
             pltpu.VMEM((2, width, group, size), BF16),
             pltpu.VMEM((2, 2, 2, size, width), F32),
             pltpu.VMEM((4, 2, size, width), F32),
-            pltpu.VMEM((2, size, width), F32),
+            pltpu.VMEM((2 * rows, width), F32),
             pltpu.VMEM((2, 2, size, width), BF16),
             pltpu.VMEM((4, 2, size, width), BF16),
             pltpu.VMEM((4, 2, size, width), BF16),
             pltpu.VMEM((2, 2, size, width), BF16),
             pltpu.VMEM((kv, 2, size, width), BF16),
-            pltpu.VMEM((2, size, width), BF16),
+            pltpu.VMEM((4, 2, size, width), BF16),
             pltpu.VMEM((4, 2, size, width), BF16),
             pltpu.VMEM((2, kv, width, size), F32),
             dma((10,)), dma((7,)), dma((7,)), dma((4, 2)), dma((2,)), dma((2,)), dma((2, 2, 2)), dma((4, 2)),
-            dma((2, 2, 2)), dma((2,)), dma((4, 2)), dma((4, 2)), dma((2,)), dma((kv, 2)), dma((2,)), dma((4, 2)),
+            dma((2, 2, 2)), dma((2,)), dma((4, 2)), dma((4, 2)), dma((2,)), dma((kv, 2)), dma((4, 2)), dma((4, 2)),
             dma((2,)), dma((2,)),
         ],
         compiler_params=pltpu.CompilerParams(

time: 30.1 us -> 29.6 us (0.983)
  the two profiles are of different devices: /device:TPU:77 before, /device:TPU:25 now
where the time goes in v5:
time: 29.6 us; the launch traced here: 29.5 us
  Pallas kernels  28.7 us (97%)
  between operations  0.8 us (3%)
    pallas_call x1, Pallas kernels, on_device(): pl.pallas_call(functools.partial(kernel, n_chips, width, group, size ** (...  27.7 us
    pallas_call x1, Pallas kernels, on_device(): pl.pallas_call(hand_over, out_shape=tuple((jax.ShapeDtypeStruct(x.shape,...  1.07 us

profile of v5, /device:TPU:25, one launch (start us, length us, event | category | flops | bytes accessed | tf_op | source)
XLA Modules:
  0.0 29.5 jit_solution(4583555843383925070)
XLA Ops:
  0.6 27.7 %shard_map.94 = (bf16[128,4,8,128]{3,2,1,0:T(8,128)(2,1)S(1)}, bf16[128,4,128]{2,1,0:T(4,128)(2,1)S(1)}, bf16[128,4,128]{2,1,0:T(4,128)(2,1)S(1)}) custom-call(bf16[128,4,8,128]{3,2,1,0:T(8,128)(2,1)} %bitcast.6, bf16[128,4,128]{2,1,0:T(4,128)(2,1)} %k_hbm.1, bf16[128,4,128]{2,1,0:T(4,128)(2,1)} %v_hbm.1, bf16[128,4,8,128]{3,2,1,0:T(8,128)(2,1)} %bitcast.7, ...), custom_call_target="tpu_custom_call" | custom-call | tf_op jit(solution)/shard_map/pallas_call | solution.py:384
  28.3 1.1 %shard_map.95 = (bf16[128,4,8,128]{3,2,1,0:T(8,128)(2,1)}, bf16[128,4,128]{2,1,0:T(4,128)(2,1)}, bf16[128,4,128]{2,1,0:T(4,128)(2,1)}) custom-call(bf16[128,4,8,128]{3,2,1,0:T(8,128)(2,1)S(1)} %get-tuple-element.9.refs_0_, bf16[128,4,128]{2,1,0:T(4,128)(2,1)S(1)} %get-tuple-element.10.refs_1_, bf16[128,4,128]{2,1,0:T(4,128)(2,1)S(1)} %get-tuple-element.11.refs_2_), custom_call_target="tpu_custom_call" | custom-call | tf_op jit(solution)/shard_map/pallas_call | solution.py:428

commit v6 on v5

--- a/solution.py
+++ b/solution.py
@@ -13,7 +13,7 @@
 NT = (((1,), (1,)), ((), ()))
 NN = (((1,), (0,)), ((), ()))
 TN = (((0,), (0,)), ((), ()))
-DIRECT = (0,)
+DIRECT = ((0, 0), (0, 1), (1, 1))
 LOG2E = 1.4426950408889634
 
 
@@ -236,8 +236,8 @@
         near[n, 1] += dv
 
     def near_done(n):
-        if n in DIRECT:
-            for p in range(2):
+        for p in range(2):
+            if (n, p) in DIRECT:
                 ret1[n, p] = near[n, p].astype(BF16)
                 give_near(n, p)
 
@@ -269,7 +269,7 @@
             def _():
                 ret2[n, p] = (part(j, a, 0) + part(j, a, 1)).astype(BF16)
 
-            if n in DIRECT:
+            if (n, p) in DIRECT:
                 copy = remote(ret2.at[n, p], rb2.at[n, p], rs2.at[n, p], rr2.at[n, p], device(-2, a))
             else:
                 copy = remote(ret2.at[n, p], pre.at[n, p], rs2.at[n, p], rp.at[n, p], device(-1, core))
@@ -326,7 +326,7 @@
     give_queries(1)
     for n in range(4):
         for p in (1, 0):
-            if n not in DIRECT:
+            if (n, p) not in DIRECT:
                 pass_on(n, p)
 
     for j in range(2):
@@ -343,7 +343,7 @@
         if True:
             arrived(rb1.at[h, p], rr1.at[h, p], has_next)
             acc = rb1[h, p].astype(F32) + (parts[0, j, p] if n % 2 == 0 else rb0[j, p].astype(F32))
-            if n in DIRECT:
+            if (n, p) in DIRECT:
                 arrived(rb2.at[n, p], rr2.at[n, p], has_next2)
                 acc = acc + rb2[n, p].astype(F32)
             total[p, h] = acc.T

time: 29.6 us -> 29.5 us (level)
  the two profiles are of different devices: /device:TPU:25 before, /device:TPU:1 now
where the time goes in v6:
time: 29.5 us; the launch traced here: 29.4 us
  Pallas kernels  28.6 us (97%)
  between operations  0.8 us (3%)
    pallas_call x1, Pallas kernels, on_device(): pl.pallas_call(functools.partial(kernel, n_chips, width, group, size ** (...  27.5 us
    pallas_call x1, Pallas kernels, on_device(): pl.pallas_call(hand_over, out_shape=tuple((jax.ShapeDtypeStruct(x.shape,...  1.07 us

profile of v6, /device:TPU:1, one launch (start us, length us, event | category | flops | bytes accessed | tf_op | source)
XLA Modules:
  0.0 29.4 jit_solution(5359124707893844529)
XLA Ops:
  0.6 27.5 %shard_map.94 = (bf16[128,4,8,128]{3,2,1,0:T(8,128)(2,1)S(1)}, bf16[128,4,128]{2,1,0:T(4,128)(2,1)S(1)}, bf16[128,4,128]{2,1,0:T(4,128)(2,1)S(1)}) custom-call(bf16[128,4,8,128]{3,2,1,0:T(8,128)(2,1)} %bitcast.6, bf16[128,4,128]{2,1,0:T(4,128)(2,1)} %k_hbm.1, bf16[128,4,128]{2,1,0:T(4,128)(2,1)} %v_hbm.1, bf16[128,4,8,128]{3,2,1,0:T(8,128)(2,1)} %bitcast.7, ...), custom_call_target="tpu_custom_call" | custom-call | tf_op jit(solution)/shard_map/pallas_call | solution.py:384
  28.1 1.1 %shard_map.95 = (bf16[128,4,8,128]{3,2,1,0:T(8,128)(2,1)}, bf16[128,4,128]{2,1,0:T(4,128)(2,1)}, bf16[128,4,128]{2,1,0:T(4,128)(2,1)}) custom-call(bf16[128,4,8,128]{3,2,1,0:T(8,128)(2,1)S(1)} %get-tuple-element.9.refs_0_, bf16[128,4,128]{2,1,0:T(4,128)(2,1)S(1)} %get-tuple-element.10.refs_1_, bf16[128,4,128]{2,1,0:T(4,128)(2,1)S(1)} %get-tuple-element.11.refs_2_), custom_call_target="tpu_custom_call" | custom-call | tf_op jit(solution)/shard_map/pallas_call | solution.py:428
